TPU v7x, 256 devices: a whole 4x4x8 slice. The times are simulated.
256 devices in a mesh: morton: 32 (over y, x, core), sub: 8 (over z).
Axes of the slice: x: 4, y: 4, z: 8, core: 2. Of those that a mesh axis runs over, the one named last changes fastest.
Arguments:
- flow_state: float32 [5, 125, 32768], P(None, None, ('morton', 'sub')), may hold values from -0.65 to 3.75, as said below
- element_level: int32 [32768], P(('morton', 'sub')), may hold values from 0 to 2
- neighbour: int32 [6, 32768], P(None, ('morton', 'sub')), may hold values from -1 to 895, as said below
- send_next: int32 [256, 32], P(('morton', 'sub')), may hold values from 0 to 767
- send_prev: int32 [256, 32], P(('morton', 'sub')), may hold values from 0 to 767
- coarse_face: int32 [256, 8, 2], P(('morton', 'sub')), may hold values from 0 to 767, as said below
- fine_face: int32 [256, 8, 2, 4], P(('morton', 'sub')), may hold values from 0 to 767
- send_count: int32 [256, 8], P(('morton', 'sub')), may hold values from 1 to 2, as said below
Outputs:
- state_out: float32 [5, 125, 32768], P(None, None, ('morton', 'sub'))
- register: float32 [5, 125, 32768], P(None, None, ('morton', 'sub'))
Inputs may be any that keep to these rules, and one draw needn't show every extreme that they name: `flow_state`: density lies in 0.7 to 1.3 and the pressure 0.4 (energy - |momentum|^2 / (2 density)) in 0.7 to 1.3 at every node. `neighbour`: an entry is -1 exactly at the slots coarse_face[k, p, j] with j < send_count[k, p]; it equals 6 * 128 + 2 * 32 + 4 (2 p + j) + q exactly at the slots fine_face[k, p, j, q] with j below the count that peer p of the sub group sends to device k; the slots of neighbours 6 * 128 to 831 are each used once; other entries are local slots. Within a device the entries of coarse_face and fine_face are distinct slots, none of them among the slots that read ghost traces. `send_count`: in every group along sub some device receives 2 used slots from every peer.
All inputs are finite; a program needn't handle non-finite values.
Results may differ from a plain program's by a relative error of at most 0.0003.
Values sent between devices are 32-bit elements; how exact they have to be, the bound alone decides.
A program may use at most 64 MiB of HBM per device.

v0:
```python
import jax
import jax.numpy as jnp
import numpy as np
from jax import lax
from jax.sharding import PartitionSpec as P

gamma_gas = 1.4
viscosity = 0.01
penalty = 0.1
lift_gain = 10.0
step_size = 0.05
section_a2 = -0.4178904745
section_b1 = 0.1496590219993
section_b2 = 0.3792103129999
highest = lax.Precision.HIGHEST


def passed_along(x, axis, by):
    devices = lax.axis_size(axis)
    return lax.ppermute(x, axis, [(i, (i + by) % devices) for i in range(devices)])


def basis_tables():
    points = np.array([-1.0, -np.sqrt(3.0 / 7.0), 0.0, np.sqrt(3.0 / 7.0), 1.0])
    weights = np.array([0.1, 49.0 / 90.0, 32.0 / 45.0, 49.0 / 90.0, 0.1])
    products = np.array(
        [np.prod([points[i] - points[m] for m in range(5) if m != i]) for i in range(5)]
    )
    derivative = np.zeros((5, 5))
    for i in range(5):
        for j in range(5):
            if i != j:
                derivative[i, j] = products[i] / (products[j] * (points[i] - points[j]))
        derivative[i, i] = -np.sum(derivative[i])
    halves = []
    projections = []
    for h in range(2):
        shifted = (points + 2.0 * h - 1.0) / 2.0
        interp = np.zeros((5, 5))
        for i in range(5):
            for j in range(5):
                interp[i, j] = np.prod(
                    [(shifted[i] - points[m]) / (points[j] - points[m]) for m in range(5) if m != j]
                )
        halves.append(interp)
        projections.append(weights[None, :] * interp.T / (2.0 * weights[:, None]))
    interpolation = np.stack([np.kron(halves[q // 2], halves[q % 2]) for q in range(4)])
    projection = np.stack([np.kron(projections[q // 2], projections[q % 2]) for q in range(4)])
    ident_five = np.eye(5)
    ident_quad = np.eye(25)
    gradients = np.stack(
        [
            np.kron(derivative, ident_quad),
            np.kron(ident_five, np.kron(derivative, ident_five)),
            np.kron(ident_quad, derivative),
        ]
    )
    laplace = (
        gradients[0] @ gradients[0] + gradients[1] @ gradients[1] + gradients[2] @ gradients[2]
    )
    select = np.zeros((6, 25, 125))
    for f in range(6):
        level = 4 * (f % 2)
        for t1 in range(5):
            for t2 in range(5):
                if f // 2 == 0:
                    node = 25 * level + 5 * t1 + t2
                elif f // 2 == 1:
                    node = 25 * t1 + 5 * level + t2
                else:
                    node = 25 * t1 + 5 * t2 + level
                select[f, 5 * t1 + t2, node] = 1.0
    return (
        jnp.asarray(derivative, jnp.float32),
        jnp.asarray(interpolation, jnp.float32),
        jnp.asarray(projection, jnp.float32),
        jnp.asarray(gradients, jnp.float32),
        jnp.asarray(laplace, jnp.float32),
        jnp.asarray(select, jnp.float32),
    )


def euler_flux(fields, d):
    density = fields[0]
    velocity = fields[1 + d] / density
    pressure = (gamma_gas - 1.0) * (
        fields[4]
        - 0.5 * (fields[1] * fields[1] + fields[2] * fields[2] + fields[3] * fields[3]) / density
    )
    components = [
        fields[1 + d],
        fields[1] * velocity,
        fields[2] * velocity,
        fields[3] * velocity,
        (fields[4] + pressure) * velocity,
    ]
    components[1 + d] = components[1 + d] + pressure
    wave_speed = jnp.abs(velocity) + jnp.sqrt(gamma_gas * pressure / density)
    return (jnp.stack(components), wave_speed)


def apply_nodes(matrix, values):
    batched = jnp.broadcast_to(matrix, (values.shape[0],) + matrix.shape)
    return jnp.einsum("fxn,fne->fxe", batched, values, precision=highest)


def volume_rate(fields, metric, gradients, laplace):
    advect = jnp.zeros_like(fields)
    for d in range(3):
        flux_d, unused = euler_flux(fields, d)
        advect = advect + apply_nodes(gradients[d], flux_d)
    diffuse = apply_nodes(laplace, fields)
    return metric * (viscosity * metric * diffuse - advect)


def face_traces(fields, select):
    return jnp.concatenate([apply_nodes(select[f], fields) for f in range(6)], axis=2)


def face_terms(traces, lookup, neighbour, metric):
    elements = metric.shape[0]
    outside_all = jnp.take(lookup, jnp.maximum(neighbour, 0), axis=2)
    normals = []
    numerics = []
    surfaces = []
    for f in range(6):
        orient = 1.0 if f % 2 else -1.0
        inside = traces[:, :, f * elements : (f + 1) * elements]
        outside = outside_all[:, :, f * elements : (f + 1) * elements]
        flux_in, speed_in = euler_flux(inside, f // 2)
        flux_out, speed_out = euler_flux(outside, f // 2)
        damping = 0.5 * jnp.maximum(speed_in, speed_out) + penalty * metric
        numeric = 0.5 * orient * (flux_in + flux_out) + damping * (inside - outside)
        coupled = neighbour[f * elements : (f + 1) * elements] >= 0
        normals.append(orient * flux_in)
        numerics.append(numeric)
        surfaces.append(jnp.where(coupled, orient * flux_in - numeric, 0.0))
    return (
        jnp.concatenate(normals, axis=2),
        jnp.concatenate(numerics, axis=2),
        jnp.concatenate(surfaces, axis=2),
    )


def lift_faces(rate_nodes, surfaces, metric, select):
    elements = metric.shape[0]
    for f in range(6):
        face_block = lift_gain * metric * surfaces[:, :, f * elements : (f + 1) * elements]
        rate_nodes = rate_nodes + apply_nodes(jnp.transpose(select[f]), face_block)
    return rate_nodes


def interpolate_panels(received, interpolation):
    panels = jnp.einsum("qus,fspj->fupjq", interpolation, received, precision=highest)
    return panels.reshape(5, 25, -1)


def project_panels(fine_fluxes, projection):
    return -jnp.einsum("qsu,fupjq->fspj", projection, fine_fluxes, precision=highest)


def coarse_terms(own_flux, returned, send_count):
    usable = jnp.arange(own_flux.shape[3])[None, :] < send_count[:, None]
    return jnp.where(usable, own_flux - returned, 0.0)


def rate_of(fields, metric, connection, tables):
    neighbour, send_next, send_prev, coarse_face, fine_face, send_count = connection
    derivative, interpolation, projection, gradients, laplace, select = tables
    traces = face_traces(fields, select)
    to_next = jnp.take(traces, send_next, axis=2)
    to_prev = jnp.take(traces, send_prev, axis=2)
    outgoing = jnp.take(traces, coarse_face, axis=2)
    from_prev = passed_along(to_next, ("morton", "sub"), 1)
    from_next = passed_along(to_prev, ("morton", "sub"), -1)
    received = lax.all_to_all(outgoing, "sub", split_axis=2, concat_axis=2, tiled=True)
    volume = volume_rate(fields, metric, gradients, laplace)
    lookup = jnp.concatenate(
        [traces, from_prev, from_next, interpolate_panels(received, interpolation)], axis=2
    )
    normals, numerics, surfaces = face_terms(traces, lookup, neighbour, metric)
    fine_fluxes = jnp.take(numerics, fine_face, axis=2)
    sent_back = lax.all_to_all(fine_fluxes, "sub", split_axis=2, concat_axis=2, tiled=True)
    returned = project_panels(sent_back, projection)
    own_flux = jnp.take(normals, coarse_face, axis=2)
    coarse_part = coarse_terms(own_flux, returned, send_count)
    surfaces = surfaces.at[:, :, coarse_face.reshape(-1)].add(coarse_part.reshape(5, 25, -1))
    return lift_faces(volume, surfaces, metric, select)


def per_device(
    flow_state, element_level, neighbour, send_next, send_prev, coarse_face, fine_face, send_count
):
    tables = basis_tables()
    metric = 0.25 * jnp.left_shift(jnp.ones_like(element_level), element_level).astype(jnp.float32)
    connection = (
        neighbour.reshape(-1),
        send_next[0],
        send_prev[0],
        coarse_face[0],
        fine_face[0],
        send_count[0],
    )
    first_section = step_size * rate_of(flow_state, metric, connection, tables)
    middle = flow_state + section_b1 * first_section
    register = section_a2 * first_section + step_size * rate_of(middle, metric, connection, tables)
    return (middle + section_b2 * register, register)


def solution(mesh):
    placed = (
        P(None, None, ("morton", "sub")),
        P(("morton", "sub")),
        P(None, ("morton", "sub")),
        P(("morton", "sub"), None),
        P(("morton", "sub"), None),
        P(("morton", "sub"), None, None),
        P(("morton", "sub"), None, None, None),
        P(("morton", "sub"), None),
    )
    return jax.shard_map(
        per_device,
        mesh=mesh,
        in_specs=placed,
        out_specs=(P(None, None, ("morton", "sub")), P(None, None, ("morton", "sub"))),
        check_vma=False,
    )
```

profile of v0, /device:TPU:0, one launch (start us, length us, event | category | flops | bytes accessed | tf_op | source)
XLA Modules:
  0.0 178.3 jit_solution(13061513388722182262)
XLA Ops:
  10.3 2.2 %copy.218 = f32[5,25,768]{1,0,2:T(8,128)} copy(f32[5,25,768]{2,1,0:T(8,128)S(1)} %get-tuple-element.276) | data formatting | bytes 768000 | tf_op jit(solution)/shard_map/concatenate | solution.py:117
  13.0 2.5 %gather_fusion.2 = f32[16,5,25]{2,1,0:T(8,128)S(1)} fusion(f32[5,25,768]{1,0,2:T(8,128)} %copy.218, s32[1024]{0:T(1024)S(1)} %get-tuple-element.295), kind=kCustom, calls=%fused_computation.1.clone | custom fusion | bytes 16064 | tf_op jit(solution)/shard_map/jit(_take)/gather | solution.py:173
  16.4 6.7 %all-to-all-start = ((f32[8,1,250]{2,1,0:T(1,128)}), f32[8,1,250]{2,1,0:T(1,128)S(1)}, u32[]{:S(2)}, u32[]{:S(2)}) async-start(f32[8,1,250]{2,1,0:T(1,128)} %reshape.327), calls=%async_computation | async-start | bytes 16384 | tf_op jit(solution)/shard_map/all_to_all | solution.py:176
  23.2 2.5 %gather_fusion = f32[32,5,25]{2,1,0:T(8,128)S(1)} fusion(f32[5,25,768]{1,0,2:T(8,128)} %copy.218, s32[1024]{0:T(1024)S(1)} %get-tuple-element.297), kind=kCustom, calls=%fused_computation.clone | custom fusion | bytes 32128 | tf_op jit(solution)/shard_map/jit(_take)/gather | solution.py:171
  25.8 2.1 %collective-permute-start = (f32[5,25,32]{2,1,0:T(8,128)S(1)}, f32[5,25,32]{2,1,0:T(8,128)S(1)}, u32[]{:S(2)}, u32[]{:S(2)}) collective-permute-start(f32[5,25,32]{2,1,0:T(8,128)S(1)} %select_bitcast_fusion.7), channel_id=1, source_target_pairs={{0,1},{1,2},{2,3},{3,4},{4,5},{5,6},{6,7},{7,8},{8,9},{9,10},{10,1... | collective-permute-start | bytes 48008 | tf_op jit(solution)/shard_map/ppermute | solution.py:20
  27.9 2.5 %gather_fusion.1 = f32[32,5,25]{2,1,0:T(8,128)S(1)} fusion(f32[5,25,768]{1,0,2:T(8,128)} %copy.218, s32[1024]{0:T(1024)S(1)} %get-tuple-element.296), kind=kCustom, calls=%fused_computation.4.clone | custom fusion | bytes 32128 | tf_op jit(solution)/shard_map/jit(_take)/gather | solution.py:172
  30.5 5.3 %collective-permute-start.1 = (f32[5,25,32]{2,1,0:T(8,128)S(1)}, f32[5,25,32]{2,1,0:T(8,128)S(1)}, u32[]{:S(2)}, u32[]{:S(2)}) collective-permute-start(f32[5,25,32]{2,1,0:T(8,128)S(1)} %select_bitcast_fusion.6), channel_id=1, source_target_pairs={{0,255},{1,0},{2,1},{3,2},{4,3},{5,4},{6,5},{7,6},{8,7},{9,8},{10,... | collective-permute-start | bytes 48008 | tf_op jit(solution)/shard_map/ppermute | solution.py:20
  41.1 2.6 %copy.230 = f32[5,25,896]{1,0,2:T(8,128)} copy(f32[5,25,896]{2,1,0:T(8,128)S(1)} %concatenate.33) | data formatting | bytes 896000 | tf_op jit(solution)/shard_map/concatenate | solution.py:178
  43.7 4.9 %gather_fusion.3 = f32[768,5,25]{2,1,0:T(8,128)} fusion(f32[5,25,896]{1,0,2:T(8,128)} %copy.230, s32[1024]{0:T(1024)S(1)} %pad_clamp_fusion.1), kind=kCustom, calls=%fused_computation.2.clone | custom fusion | bytes 771072 | tf_op jit(solution)/shard_map/jit(_take)/gather | solution.py:122
  48.6 2.2 %copy.231 = f32[768,5,25]{0,2,1:T(8,128)S(1)} copy(f32[768,5,25]{2,1,0:T(8,128)} %gather_fusion.3) | data formatting | bytes 768000 | tf_op jit(solution)/shard_map/jit(_take)/gather | solution.py:122
  52.1 2.2 %copy.239 = f32[5,25,768]{1,0,2:T(8,128)} copy(f32[5,25,768]{2,1,0:T(8,128)S(1)} %get-tuple-element.72) | data formatting | bytes 768000 | tf_op jit(solution)/shard_map/concatenate | solution.py:140
  54.3 2.5 %gather_fusion.5 = f32[64,5,25]{2,1,0:T(8,128)S(1)} fusion(f32[5,25,768]{1,0,2:T(8,128)} %copy.239, s32[1024]{0:T(1024)S(1)} %get-tuple-element.294), kind=kCustom, calls=%fused_computation.3.clone | custom fusion | bytes 64256 | tf_op jit(solution)/shard_map/jit(_take)/gather | solution.py:182
  57.8 3.5 %all-to-all-start.1 = ((f32[8,1,1000]{2,1,0:T(1,128)}), f32[8,1,1000]{2,1,0:T(1,128)S(1)}, u32[]{:S(2)}, u32[]{:S(2)}) async-start(f32[8,1,1000]{2,1,0:T(1,128)} %reshape.329), calls=%async_computation.1 | async-start | bytes 65536 | tf_op jit(solution)/shard_map/all_to_all | solution.py:183
  61.6 2.2 %copy.234 = f32[5,25,768]{1,0,2:T(8,128)} copy(f32[5,25,768]{2,1,0:T(8,128)S(1)} %get-tuple-element.226) | data formatting | bytes 768000 | tf_op jit(solution)/shard_map/concatenate | solution.py:139
  63.8 2.5 %gather_fusion.4 = f32[16,5,25]{2,1,0:T(8,128)S(1)} fusion(f32[5,25,768]{1,0,2:T(8,128)} %copy.234, s32[1024]{0:T(1024)S(1)} %get-tuple-element.295), kind=kCustom, calls=%fused_computation.7.clone | custom fusion | bytes 16064 | tf_op jit(solution)/shard_map/jit(_take)/gather | solution.py:185
  66.3 2.2 %copy.244 = f32[5,25,768]{1,0,2:T(8,128)} copy(f32[5,25,768]{2,1,0:T(8,128)S(1)} %constant_dynamic-update-slice_fusion.81) | data formatting | bytes 768000 | tf_op jit(solution)/shard_map/concatenate | solution.py:141
  70.3 2.1 %scatter_fusion = f32[5,25,768]{1,0,2:T(8,128)} fusion(f32[5,25,768]{1,0,2:T(8,128)} %copy.244, s32[16]{0:T(128)S(1)} %fusion.114, f32[16,5,25]{2,1,0:T(8,128)S(1)} %copy.245), kind=kCustom, calls=%fused_computation.12 | custom fusion | flops 2000 | bytes 24064 | tf_op jit(solution)/shard_map/scatter-add | solution.py:187
  72.4 2.8 %fusion.128 = (f32[5,25,128]{1,0,2:T(8,128)S(1)}, f32[5,25,128]{1,0,2:T(8,128)S(1)}, f32[5,25,128]{1,0,2:T(8,128)S(1)}, f32[5,25,128]{1,0,2:T(8,128)S(1)}, f32[5,25,128]{1,0,2:T(8,128)S(1)}, /*index=5*/f32[5,25,128]{1,0,2:T(8,128)}) fusion(f32[5,25,768]{1,0,2:T(8,128)} %scatter_fusion), kind=kLoop, calls=%fused_computation.522 | loop fusion | bytes 768000 | tf_op jit(solution)/shard_map/slice | solution.py:148
  90.1 2.2 %copy.260 = f32[5,25,768]{1,0,2:T(8,128)S(1)} copy(f32[5,25,768]{2,1,0:T(8,128)} %copy-done.17) | data formatting | bytes 768000 | tf_op jit(solution)/shard_map/concatenate | solution.py:117
  96.2 6.4 %all-to-all-start.2 = ((f32[8,1,250]{2,1,0:T(1,128)}), f32[8,1,250]{2,1,0:T(1,128)S(1)}, u32[]{:S(2)}, u32[]{:S(2)}) async-start(f32[8,1,250]{2,1,0:T(1,128)} %reshape.331), calls=%async_computation.2 | async-start | bytes 16384 | tf_op jit(solution)/shard_map/all_to_all | solution.py:176
  104.2 5.0 %collective-permute-start.3 = (f32[5,25,32]{2,1,0:T(8,128)S(1)}, f32[5,25,32]{2,1,0:T(8,128)S(1)}, u32[]{:S(2)}, u32[]{:S(2)}) collective-permute-start(f32[5,25,32]{2,1,0:T(8,128)S(1)} %select_bitcast_fusion.4), channel_id=1, source_target_pairs={{0,255},{1,0},{2,1},{3,2},{4,3},{5,4},{6,5},{7,6},{8,7},{9,8},{10,... | collective-permute-start | bytes 48008 | tf_op jit(solution)/shard_map/ppermute | solution.py:20
  115.9 4.5 %collective-permute-done.2 = f32[5,25,32]{2,1,0:T(8,128)S(1)} collective-permute-done((f32[5,25,32]{2,1,0:T(8,128)S(1)}, f32[5,25,32]{2,1,0:T(8,128)S(1)}, u32[]{:S(2)}, u32[]{:S(2)}) %collective-permute-start.2) | collective-permute-done | bytes 16032 | tf_op jit(solution)/shard_map/ppermute | solution.py:20
  120.6 2.6 %copy.272 = f32[5,25,896]{1,0,2:T(8,128)} copy(f32[5,25,896]{2,1,0:T(8,128)S(1)} %concatenate.38) | data formatting | bytes 896000 | tf_op jit(solution)/shard_map/concatenate | solution.py:178
  123.2 3.3 %gather_fusion.9 = f32[768,5,25]{2,1,0:T(8,128)S(1)} fusion(f32[5,25,896]{1,0,2:T(8,128)} %copy.272, s32[1024]{0:T(1024)} %copy-done.56), kind=kCustom, calls=%fused_computation.10.clone | custom fusion | bytes 771072 | tf_op jit(solution)/shard_map/jit(_take)/gather | solution.py:122
  141.3 2.2 %copy.280 = f32[5,25,768]{1,0,2:T(8,128)} copy(f32[5,25,768]{2,1,0:T(8,128)S(1)} %get-tuple-element.17) | data formatting | bytes 768000 | tf_op jit(solution)/shard_map/concatenate | solution.py:140
  143.6 2.5 %gather_fusion.11 = f32[64,5,25]{2,1,0:T(8,128)S(1)} fusion(f32[5,25,768]{1,0,2:T(8,128)} %copy.280, s32[1024]{0:T(1024)S(1)} %copy-done.34), kind=kCustom, calls=%fused_computation.11.clone | custom fusion | bytes 64256 | tf_op jit(solution)/shard_map/jit(_take)/gather | solution.py:182
  147.1 4.2 %all-to-all-start.3 = ((f32[8,1,1000]{2,1,0:T(1,128)}), f32[8,1,1000]{2,1,0:T(1,128)}, u32[]{:S(2)}, u32[]{:S(2)}) async-start(f32[8,1,1000]{2,1,0:T(1,128)} %reshape.333), calls=%async_computation.3 | async-start | bytes 65536 | tf_op jit(solution)/shard_map/all_to_all | solution.py:183
  152.3 2.2 %copy.275 = f32[5,25,768]{1,0,2:T(8,128)S(1)} copy(f32[5,25,768]{2,1,0:T(8,128)} %copy-done.18) | data formatting | bytes 768000 | tf_op jit(solution)/shard_map/concatenate | solution.py:139
  155.1 2.2 %copy.285 = f32[5,25,768]{1,0,2:T(8,128)S(1)} copy(f32[5,25,768]{2,1,0:T(8,128)} %copy-done.19) | data formatting | bytes 768000 | tf_op jit(solution)/shard_map/concatenate | solution.py:141
  157.3 1.8 all-to-all-done.3
  159.1 2.0 %reduce.3 = f32[8,1000]{1,0:T(8,128)} reduce(f32[8,1,1000]{2,1,0:T(1,128)} %all-to-all-done.3, f32[]{:T(128)} %broadcast.738), dimensions={1}, to_apply=%all_to_all.15.reduce_sub_computation | reduce | bytes 64004 | tf_op jit(solution)/shard_map/all_to_all | solution.py:183
  165.0 1.7 fusion.127
  (446 shorter events, 78.6 us)
Async XLA Ops:
  2.0 67.9 %copy-start.79 = (pred[8,2]{0,1:T(4,128)(4,1)}, pred[8,2]{0,1:T(4,128)(4,1)S(1)}, u32[]{:S(2)}) copy-start(pred[8,2]{0,1:T(4,128)(4,1)S(1)} %compare_and_fusion.2) | copy-start | bytes 52
  6.1 17.0 %copy-start.88 = (s32[1,32]{1,0:T(1,128)S(1)}, s32[1,32]{1,0:T(1,128)}, u32[]{:S(2)}) copy-start(s32[1,32]{1,0:T(1,128)} %param.24) | copy-start | bytes 388
  6.1 17.0 %copy-start.89 = (s32[1,32]{1,0:T(1,128)S(1)}, s32[1,32]{1,0:T(1,128)}, u32[]{:S(2)}) copy-start(s32[1,32]{1,0:T(1,128)} %param.25) | copy-start | bytes 388
  10.3 25.5 %copy-start.59 = (s32[6,128]{1,0:T(8,128)S(1)}, s32[6,128]{1,0:T(8,128)}, u32[]{:S(2)}) copy-start(s32[6,128]{1,0:T(8,128)} %param.23) | copy-start | bytes 9220
  10.3 25.6 %copy-start.78 = (s32[1,8,2]{1,2,0:T(2,128)S(1)}, s32[1,8,2]{1,2,0:T(2,128)}, u32[]{:S(2)}) copy-start(s32[1,8,2]{1,2,0:T(2,128)} %param.26) | copy-start | bytes 196
  10.3 25.7 %copy-start = (f32[5,125,128]{2,1,0:T(8,128)S(1)}, f32[5,125,128]{2,1,0:T(8,128)}, u32[]{:S(2)}) copy-start(f32[5,125,128]{2,1,0:T(8,128)} %param.21) | copy-start | bytes 960004
  10.3 25.7 %copy-start.87 = (s32[128]{0:T(128)S(1)}, s32[128]{0:T(128)}, u32[]{:S(2)}) copy-start(s32[128]{0:T(128)} %param.22) | copy-start | bytes 1540
  10.3 25.8 %copy-start.90 = (s32[1,8]{1,0:T(1,128)S(1)}, s32[1,8]{1,0:T(1,128)}, u32[]{:S(2)}) copy-start(s32[1,8]{1,0:T(1,128)} %param.28) | copy-start | bytes 100
  12.6 23.9 %copy-start.29 = (f32[125,125]{1,0:T(8,128)S(1)}, f32[125,125]{1,0:T(8,128)}, u32[]{:S(2)}) copy-start(f32[125,125]{1,0:T(8,128)} %constant.132) | copy-start | bytes 187504
  12.9 41.4 %copy-start.33 = (s32[1024]{0:T(1024)}, s32[1024]{0:T(1024)S(1)}, u32[]{:S(2)}) copy-start(s32[1024]{0:T(1024)S(1)} %get-tuple-element.294) | copy-start | bytes 12292
  12.9 79.3 %copy-start.31 = (s32[1024]{0:T(1024)}, s32[1024]{0:T(1024)S(1)}, u32[]{:S(2)}) copy-start(s32[1024]{0:T(1024)S(1)} %get-tuple-element.295) | copy-start | bytes 12292
  13.0 23.9 %copy-start.25 = (f32[125,125]{1,0:T(8,128)S(1)}, f32[125,125]{1,0:T(8,128)}, u32[]{:S(2)}) copy-start(f32[125,125]{1,0:T(8,128)} %constant.134) | copy-start | bytes 187504
  15.5 21.8 %copy-start.23 = (f32[125,125]{1,0:T(8,128)S(1)}, f32[125,125]{1,0:T(8,128)}, u32[]{:S(2)}) copy-start(f32[125,125]{1,0:T(8,128)} %constant.136) | copy-start | bytes 187504
  16.4 22.7 %all-to-all-start = ((f32[8,1,250]{2,1,0:T(1,128)}), f32[8,1,250]{2,1,0:T(1,128)S(1)}, u32[]{:S(2)}, u32[]{:S(2)}) async-start(f32[8,1,250]{2,1,0:T(1,128)} %reshape.327), calls=%async_computation | async-start | bytes 16384 | tf_op jit(solution)/shard_map/all_to_all | solution.py:176
  25.8 15.1 %collective-permute-start = (f32[5,25,32]{2,1,0:T(8,128)S(1)}, f32[5,25,32]{2,1,0:T(8,128)S(1)}, u32[]{:S(2)}, u32[]{:S(2)}) collective-permute-start(f32[5,25,32]{2,1,0:T(8,128)S(1)} %select_bitcast_fusion.7), channel_id=1, source_target_pairs={{0,1},{1,2},{2,3},{3,4},{4,5},{5,6},{6,7},{7,8},{8,9},{9,10},{10,1... | collective-permute-start | bytes 48008 | tf_op jit(solution)/shard_map/ppermute | solution.py:20
  30.5 10.4 %collective-permute-start.1 = (f32[5,25,32]{2,1,0:T(8,128)S(1)}, f32[5,25,32]{2,1,0:T(8,128)S(1)}, u32[]{:S(2)}, u32[]{:S(2)}) collective-permute-start(f32[5,25,32]{2,1,0:T(8,128)S(1)} %select_bitcast_fusion.6), channel_id=1, source_target_pairs={{0,255},{1,0},{2,1},{3,2},{4,3},{5,4},{6,5},{7,6},{8,7},{9,8},{10,... | collective-permute-start | bytes 48008 | tf_op jit(solution)/shard_map/ppermute | solution.py:20
  35.8 25.5 %copy-start.76 = (pred[128]{0:T(512)(128)(4,1)}, pred[128]{0:T(512)(128)(4,1)S(1)}, u32[]{:S(2)}) copy-start(pred[128]{0:T(512)(128)(4,1)S(1)} %get-tuple-element.260) | copy-start | bytes 388
  35.8 25.5 %copy-start.74 = (pred[128]{0:T(512)(128)(4,1)}, pred[128]{0:T(512)(128)(4,1)S(1)}, u32[]{:S(2)}) copy-start(pred[128]{0:T(512)(128)(4,1)S(1)} %get-tuple-element.259) | copy-start | bytes 388
  35.9 25.6 %copy-start.72 = (pred[128]{0:T(512)(128)(4,1)}, pred[128]{0:T(512)(128)(4,1)S(1)}, u32[]{:S(2)}) copy-start(pred[128]{0:T(512)(128)(4,1)S(1)} %get-tuple-element.258) | copy-start | bytes 388
  35.9 25.6 %copy-start.70 = (pred[128]{0:T(512)(128)(4,1)}, pred[128]{0:T(512)(128)(4,1)S(1)}, u32[]{:S(2)}) copy-start(pred[128]{0:T(512)(128)(4,1)S(1)} %get-tuple-element.257) | copy-start | bytes 388
  35.9 25.6 %copy-start.68 = (pred[128]{0:T(512)(128)(4,1)}, pred[128]{0:T(512)(128)(4,1)S(1)}, u32[]{:S(2)}) copy-start(pred[128]{0:T(512)(128)(4,1)S(1)} %get-tuple-element.261) | copy-start | bytes 388
  35.9 25.6 %copy-start.66 = (pred[128]{0:T(512)(128)(4,1)}, pred[128]{0:T(512)(128)(4,1)S(1)}, u32[]{:S(2)}) copy-start(pred[128]{0:T(512)(128)(4,1)S(1)} %get-tuple-element.256) | copy-start | bytes 388
  36.1 45.7 %copy-start.35 = (f32[128]{0:T(128)}, f32[128]{0:T(128)S(1)}, u32[]{:S(2)}) copy-start(f32[128]{0:T(128)S(1)} %get-tuple-element.262) | copy-start | bytes 1540
  36.1 33.8 %copy-start.83 = (pred[8,2]{0,1:T(4,128)(4,1)}, pred[8,2]{0,1:T(4,128)(4,1)S(1)}, u32[]{:S(2)}) copy-start(pred[8,2]{0,1:T(4,128)(4,1)S(1)} %iota_compare_fusion) | copy-start | bytes 52
  36.2 34.1 %copy-start.81 = (s32[16]{0:T(128)}, s32[16]{0:T(128)S(1)}, u32[]{:S(2)}) copy-start(s32[16]{0:T(128)S(1)} %fusion.114) | copy-start | bytes 196
  39.1 17.8 %copy-start.57 = (pred[8,2,4]{2,1,0:T(4,128)(4,1)}, pred[8,2,4]{2,1,0:T(4,128)(4,1)S(1)}, u32[]{:S(2)}) copy-start(pred[8,2,4]{2,1,0:T(4,128)(4,1)S(1)} %copy.237) | copy-start | bytes 196
  57.8 11.3 %all-to-all-start.1 = ((f32[8,1,1000]{2,1,0:T(1,128)}), f32[8,1,1000]{2,1,0:T(1,128)S(1)}, u32[]{:S(2)}, u32[]{:S(2)}) async-start(f32[8,1,1000]{2,1,0:T(1,128)} %reshape.329), calls=%async_computation.1 | async-start | bytes 65536 | tf_op jit(solution)/shard_map/all_to_all | solution.py:183
  95.3 16.9 %copy-start.24 = (f32[125,125]{1,0:T(8,128)S(1)}, f32[125,125]{1,0:T(8,128)}, u32[]{:S(2)}) copy-start(f32[125,125]{1,0:T(8,128)} %constant.136) | copy-start | bytes 187504
  96.2 18.4 %all-to-all-start.2 = ((f32[8,1,250]{2,1,0:T(1,128)}), f32[8,1,250]{2,1,0:T(1,128)S(1)}, u32[]{:S(2)}, u32[]{:S(2)}) async-start(f32[8,1,250]{2,1,0:T(1,128)} %reshape.331), calls=%async_computation.2 | async-start | bytes 16384 | tf_op jit(solution)/shard_map/all_to_all | solution.py:176
  104.2 11.6 %collective-permute-start.3 = (f32[5,25,32]{2,1,0:T(8,128)S(1)}, f32[5,25,32]{2,1,0:T(8,128)S(1)}, u32[]{:S(2)}, u32[]{:S(2)}) collective-permute-start(f32[5,25,32]{2,1,0:T(8,128)S(1)} %select_bitcast_fusion.4), channel_id=1, source_target_pairs={{0,255},{1,0},{2,1},{3,2},{4,3},{5,4},{6,5},{7,6},{8,7},{9,8},{10,... | collective-permute-start | bytes 48008 | tf_op jit(solution)/shard_map/ppermute | solution.py:20
  111.0 9.4 %collective-permute-start.2 = (f32[5,25,32]{2,1,0:T(8,128)S(1)}, f32[5,25,32]{2,1,0:T(8,128)S(1)}, u32[]{:S(2)}, u32[]{:S(2)}) collective-permute-start(f32[5,25,32]{2,1,0:T(8,128)S(1)} %select_bitcast_fusion.5), channel_id=1, source_target_pairs={{0,1},{1,2},{2,3},{3,4},{4,5},{5,6},{6,7},{7,8},{8,9},{9,10},{10,1... | collective-permute-start | bytes 48008 | tf_op jit(solution)/shard_map/ppermute | solution.py:20
  147.1 12.0 %all-to-all-start.3 = ((f32[8,1,1000]{2,1,0:T(1,128)}), f32[8,1,1000]{2,1,0:T(1,128)}, u32[]{:S(2)}, u32[]{:S(2)}) async-start(f32[8,1,1000]{2,1,0:T(1,128)} %reshape.333), calls=%async_computation.3 | async-start | bytes 65536 | tf_op jit(solution)/shard_map/all_to_all | solution.py:183
  (67 other events, 524.2 us)
where the time goes:
time: 181 us; the launch traced here: 178 us
  local copies, waits for them, and re-layouts  79.5 us (44%)
  starting transfers between devices  33.4 us (18%)
  matrix products  32.2 us (18%)
  other arithmetic  23.2 us (13%)
  waiting for transfers between devices  6.88 us (4%)
  between operations  3.11 us (2%)
    dot_general x32, matrix products, apply_nodes(): return jnp.einsum('fxn,fne->fxe', batched, values, precision=highest)  29.9 us
    unnamed x213, local copies, waits for them, and re-layouts  17.2 us
    all_to_all x2, starting transfers between devices, rate_of(): lax.all_to_all(outgoing, 'sub', split_axis=2, concat_axis=2, tiled=True)  13.1 us
    ppermute x4, starting transfers between devices, passed_along(): lax.ppermute(x, axis, [(i, (i + by) % devices) for i in range(devices)])  12.5 us
    gather x4, local copies, waits for them, and re-layouts, face_terms(): outside_all = jnp.take(lookup, jnp.maximum(neighbour, 0), axis=2)  12.1 us
    all_to_all x2, starting transfers between devices, rate_of(): lax.all_to_all(fine_fluxes, 'sub', split_axis=2, concat_axis=2, tiled=True)  7.73 us
    unnamed x104, other arithmetic  7.65 us
    concatenate x4, local copies, waits for them, and re-layouts, rate_of(): jnp.concatenate([traces, from_prev, from_next, interpolate_panels(receive...  5.49 us
  transfers between devices with their start and end apart: 8, of which 3 were waited for; matrix products, arithmetic and copies ran while one was open for 17% of the time, Pallas kernels for 0%

commit v1 on v0

v1 whole, which is shorter than its diff:
```python
import functools

import jax
import jax.numpy as jnp
import numpy as np
from jax import lax
from jax.experimental import pallas as pl
from jax.experimental.pallas import tpu as pltpu
from jax.sharding import PartitionSpec as P

gamma_gas = 1.4
viscosity = 0.01
penalty = 0.1
lift_gain = 10.0
step_size = 0.05
section_a2 = -0.4178904745
section_b1 = 0.1496590219993
section_b2 = 0.3792103129999
MESH = pl.DeviceIdType.MESH
f32 = jnp.float32
bf16 = jnp.bfloat16


def basis_tables():
    points = np.array([-1.0, -np.sqrt(3.0 / 7.0), 0.0, np.sqrt(3.0 / 7.0), 1.0])
    weights = np.array([0.1, 49.0 / 90.0, 32.0 / 45.0, 49.0 / 90.0, 0.1])
    products = np.array(
        [np.prod([points[i] - points[m] for m in range(5) if m != i]) for i in range(5)]
    )
    derivative = np.zeros((5, 5))
    for i in range(5):
        for j in range(5):
            if i != j:
                derivative[i, j] = products[i] / (products[j] * (points[i] - points[j]))
        derivative[i, i] = -np.sum(derivative[i])
    halves = []
    projections = []
    for h in range(2):
        shifted = (points + 2.0 * h - 1.0) / 2.0
        interp = np.zeros((5, 5))
        for i in range(5):
            for j in range(5):
                interp[i, j] = np.prod(
                    [(shifted[i] - points[m]) / (points[j] - points[m]) for m in range(5) if m != j]
                )
        halves.append(interp)
        projections.append(weights[None, :] * interp.T / (2.0 * weights[:, None]))
    interpolation = np.stack([np.kron(halves[q // 2], halves[q % 2]) for q in range(4)])
    projection = np.stack([np.kron(projections[q // 2], projections[q % 2]) for q in range(4)])
    ident_five = np.eye(5)
    ident_quad = np.eye(25)
    gradients = np.stack(
        [
            np.kron(derivative, ident_quad),
            np.kron(ident_five, np.kron(derivative, ident_five)),
            np.kron(ident_quad, derivative),
        ]
    )
    laplace = (
        gradients[0] @ gradients[0] + gradients[1] @ gradients[1] + gradients[2] @ gradients[2]
    )
    return interpolation, projection, gradients, laplace


def two_parts(table):
    table = table.astype(np.float32)
    high = table.astype(jnp.bfloat16)
    low = (table - high.astype(np.float32)).astype(jnp.bfloat16)
    return np.stack([high, low])


def operator_tables():
    interpolation, projection, gradients, laplace = basis_tables()
    volume = np.zeros((128, 512))
    for d in range(3):
        volume[:125, 128 * d : 128 * d + 125] = -gradients[d]
    volume[:125, 384:509] = laplace
    panel = np.zeros((128, 512))
    gather = np.zeros((512, 128))
    for q in range(4):
        for f in range(5):
            rows = slice(25 * f, 25 * f + 25)
            columns = slice(128 * q + 25 * f, 128 * q + 25 * f + 25)
            panel[rows, columns] = interpolation[q].T
            gather[columns, rows] = projection[q].T
    return two_parts(volume).reshape(256, 512), two_parts(panel), two_parts(gather)


def split(x):
    high = x.astype(bf16)
    low = (x - high.astype(f32)).astype(bf16)
    return high, low


def dot(a, b):
    return jnp.dot(a, b, preferred_element_type=f32)


def gas_state(fields):
    inverse = 1.0 / fields[0]
    kinetic = fields[1] * fields[1] + fields[2] * fields[2] + fields[3] * fields[3]
    pressure = (gamma_gas - 1.0) * (fields[4] - 0.5 * kinetic * inverse)
    return inverse, pressure


def flux_along(fields, d, inverse, pressure):
    velocity = fields[1 + d] * inverse
    components = [
        fields[1 + d],
        fields[1] * velocity,
        fields[2] * velocity,
        fields[3] * velocity,
        (fields[4] + pressure) * velocity,
    ]
    components[1 + d] = components[1 + d] + pressure
    return components, velocity


def sound_speed(inverse, pressure):
    return jnp.sqrt(gamma_gas * pressure * inverse)


def kernel(
    n_morton,
    n_sub,
    state_ref,
    level_ref,
    near_ref,
    next_ref,
    prev_ref,
    coarse_ref,
    fine_ref,
    count_ref,
    volume_ref,
    panel_ref,
    gather_ref,
    out_ref,
    register_ref,
    x_ref,
    rate_ref,
    first_ref,
    face_ref,
    face_bf_ref,
    rows_ref,
    pick_ref,
    spread_ref,
    outside_ref,
    added_ref,
    flux_high_ref,
    flux_low_ref,
    mortar_ref,
    numeric_ref,
    ring_send,
    ring_recv,
    message_send,
    message_recv,
    send_sem,
    recv_sem,
):
    m = lax.axis_index("morton")
    s = lax.axis_index("sub")
    devices = n_morton * n_sub
    place = m * n_sub + s
    after = lax.rem(place + 1, devices)
    before = lax.rem(place + devices - 1, devices)
    after_id = (after // n_sub, lax.rem(after, n_sub))
    before_id = (before // n_sub, lax.rem(before, n_sub))
    peers = [lax.rem(s + o, n_sub) for o in range(n_sub)]

    barrier = pltpu.get_barrier_semaphore()
    for o in range(1, n_sub):
        pl.semaphore_signal(barrier, inc=1, device_id=(m, peers[o]), device_id_type=MESH)
    for target in (after_id, before_id):
        pl.semaphore_signal(barrier, inc=1, device_id=target, device_id_type=MESH)

    level = level_ref[...]
    metric = 0.25 * jnp.left_shift(jnp.ones_like(level), level).astype(f32)
    near = near_ref[...]
    extra = near - 832
    panel_lane = 832 + (extra & 3) * 16 + ((extra >> 2) & 1) * 8 + (extra >> 3)
    entry = jnp.where(near >= 832, panel_lane, near)

    for f in range(5):
        x_ref[f, 0:125, :] = state_ref[f]
        x_ref[f, 125:128, :] = jnp.ones((3, 128), f32)
    row_ids = lax.broadcasted_iota(jnp.int32, (128, 128), 0)
    for face in range(6):
        face_ref[face, 125:126, :] = jnp.full((1, 128), float(face // 2), f32)
        face_ref[face, 126:127, :] = metric
        face_ref[face, 127:128, :] = jnp.full((1, 128), 1.0 if face % 2 else -1.0, f32)
    numeric_ref[125:128, :] = jnp.zeros((3, 128), f32)

    def section(step):
        for face in range(6):
            level_at = 4 * (face % 2)
            for f in range(5):
                base = 25 * f
                if face < 2:
                    face_ref[face, base : base + 25, :] = x_ref[f, 25 * level_at : 25 * level_at + 25, :]
                elif face < 4:
                    for a in range(5):
                        start = 25 * a + 5 * level_at
                        face_ref[face, base + 5 * a : base + 5 * a + 5, :] = x_ref[f, start : start + 5, :]
                else:
                    face_ref[face, base : base + 25, :] = x_ref[f, pl.ds(level_at, 25, stride=5), :]
        for face in range(6):
            rows_ref[128 * face : 128 * face + 128, :] = face_ref[face].T

        if step == 0:
            pl.semaphore_wait(barrier, n_sub + 1)
        copies = []
        for p in range(n_sub):
            for j in range(2):
                for q in range(4):
                    message_send[step, p, 4 * j + q : 4 * j + q + 1, :] = rows_ref[
                        pl.ds(fine_ref[0, p, j, q], 1), :
                    ]
                message_send[step, p, 8 + j : 9 + j, :] = rows_ref[pl.ds(coarse_ref[0, p, j], 1), :]
        for o in (4, 3, 5, 2, 6, 1, 7):
            copy = pltpu.make_async_remote_copy(
                src_ref=message_send.at[step, peers[o]],
                dst_ref=message_recv.at[step, s],
                send_sem=send_sem.at[step, o],
                recv_sem=recv_sem.at[step, o],
                device_id=(m, peers[o]),
                device_id_type=MESH,
            )
            copy.start()
            copies.append(copy)
        for side, (list_ref, target) in enumerate(((next_ref, after_id), (prev_ref, before_id))):
            for i in range(32):
                ring_send[step, side, i : i + 1, :] = rows_ref[pl.ds(list_ref[0, i], 1), :]
            copy = pltpu.make_async_remote_copy(
                src_ref=ring_send.at[step, side],
                dst_ref=ring_recv.at[step, side],
                send_sem=send_sem.at[step, n_sub + side],
                recv_sem=recv_sem.at[step, n_sub + side],
                device_id=target,
                device_id_type=MESH,
            )
            copy.start()
            copies.append(copy)
        message_recv[step, s] = message_send[step, s]

        fields = [x_ref[f] for f in range(5)]
        inverse, pressure = gas_state(fields)
        for d in range(3):
            components, unused = flux_along(fields, d, inverse, pressure)
            for f in range(5):
                high, low = split(components[f])
                flux_high_ref[128 * d : 128 * d + 128, 128 * f : 128 * f + 128] = high
                flux_low_ref[128 * d : 128 * d + 128, 128 * f : 128 * f + 128] = low
        for f in range(5):
            high, low = split(viscosity * metric * fields[f])
            flux_high_ref[384:512, 128 * f : 128 * f + 128] = high
            flux_low_ref[384:512, 128 * f : 128 * f + 128] = low
        both = dot(volume_ref[...], flux_high_ref[...])
        total = both[0:128] + both[128:256] + dot(volume_ref[0:128, :], flux_low_ref[...])
        for f in range(5):
            rate_ref[f] = metric * total[:, 128 * f : 128 * f + 128]

        if step == 0:
            for face in range(6):
                wanted = entry[face : face + 1, :]
                for block in range(7):
                    hit = (row_ids + 128 * block) == wanted
                    pick_ref[128 * block : 128 * block + 128, 128 * face : 128 * face + 128] = jnp.where(
                        hit, 1.0, 0.0
                    ).astype(bf16)
            small_rows = lax.broadcasted_iota(jnp.int32, (16, 128), 0)
            small_lanes = lax.broadcasted_iota(jnp.int32, (16, 128), 1)
            owner = jnp.full((16, 128), -1, jnp.int32)
            for j in range(2):
                for p in range(n_sub):
                    slot = jnp.where(j < count_ref[0, p], coarse_ref[0, p, j], -1)
                    owner = jnp.where(small_rows == 8 * j + p, slot, owner)
            for face in range(6):
                spread_ref[:, 128 * face : 128 * face + 128] = jnp.where(
                    owner == small_lanes + 128 * face, 1.0, 0.0
                ).astype(bf16)
            owners.append(owner)
        for face in range(6):
            high, low = split(face_ref[face])
            face_bf_ref[0:128, 128 * face : 128 * face + 128] = high
            face_bf_ref[128:256, 128 * face : 128 * face + 128] = low
        local = dot(face_bf_ref[...], pick_ref[0:768, :])
        local = local[0:128] + local[128:256]
        for face in range(6):
            outside_ref[face] = local[:, 128 * face : 128 * face + 128]

        def panels_of(source):
            coarse_rows = jnp.concatenate(
                [source[step, :, 8 + j, :] for j in range(2)], axis=0
            )
            high, low = split(coarse_rows)
            wide = dot(high, panel_ref[0]) + dot(low, panel_ref[0]) + dot(high, panel_ref[1])
            return [wide[:, 128 * q : 128 * q + 128] for q in range(4)]

        own_panels = panels_of(message_send)

        for copy in copies:
            copy.wait_recv()

        arrived = jnp.concatenate(
            [ring_recv[step, 0], ring_recv[step, 1]] + panels_of(message_recv), axis=0
        ).T
        high, low = split(arrived)
        remote = dot(jnp.concatenate([high, low], axis=0), pick_ref[768:896, :])
        remote = remote[0:128] + remote[128:256]
        for face in range(6):
            outside_ref[face] = outside_ref[face] + remote[:, 128 * face : 128 * face + 128]

        fine_rows = [
            message_recv[step, :, 4 * j + q, :] for q in range(4) for j in range(2)
        ]
        mortar_ref[...] = jnp.concatenate(fine_rows + own_panels, axis=0).T
        left = lax.broadcasted_iota(jnp.int32, (1, 128), 1) < 64

        def across(x):
            return pltpu.roll(x, 64, 1)

        facts = [mortar_ref[125 + i : 126 + i, :] for i in range(3)]
        facts = [jnp.where(left, x, across(x)) for x in facts]
        along, mortar_metric, orient = facts
        sides = [mortar_ref[25 * f : 25 * f + 25, :] for f in range(5)]
        inverse, pressure = gas_state(sides)
        normal = jnp.where(along < 0.5, sides[1], jnp.where(along < 1.5, sides[2], sides[3]))
        velocity = normal * inverse
        speed = jnp.abs(velocity) + sound_speed(inverse, pressure)
        components = [
            normal,
            sides[1] * velocity + jnp.where(along < 0.5, pressure, 0.0),
            sides[2] * velocity + jnp.where((along > 0.5) & (along < 1.5), pressure, 0.0),
            sides[3] * velocity + jnp.where(along > 1.5, pressure, 0.0),
            (sides[4] + pressure) * velocity,
        ]
        damping = 0.5 * jnp.maximum(speed, across(speed)) + penalty * mortar_metric
        for f in range(5):
            numeric_ref[25 * f : 25 * f + 25, :] = 0.5 * orient * (
                components[f] + across(components[f])
            ) + damping * (sides[f] - across(sides[f]))
        numeric = numeric_ref[...].T
        wide = jnp.concatenate([numeric[16 * q : 16 * q + 16, :] for q in range(4)], axis=1)
        high, low = split(wide)
        projected = dot(high, gather_ref[0]) + dot(low, gather_ref[0]) + dot(high, gather_ref[1])
        projected = jnp.where(owners[0] >= 0, projected, 0.0).T
        high, low = split(projected)
        added = dot(jnp.concatenate([high, low], axis=0), spread_ref[...])
        added = added[0:128] + added[128:256]
        for face in range(6):
            added_ref[face] = added[:, 128 * face : 128 * face + 128]

        gain = lift_gain * metric
        for face in range(6):
            d = face // 2
            orient_here = 1.0 if face % 2 else -1.0
            inside = [face_ref[face, 25 * f : 25 * f + 25, :] for f in range(5)]
            beyond = [outside_ref[face, 25 * f : 25 * f + 25, :] for f in range(5)]
            coupled = near[face : face + 1, :] >= 0
            beyond = [jnp.where(coupled, b, i) for b, i in zip(beyond, inside)]
            inverse, pressure = gas_state(inside)
            flux_in, velocity = flux_along(inside, d, inverse, pressure)
            speed_in = jnp.abs(velocity) + sound_speed(inverse, pressure)
            inverse, pressure = gas_state(beyond)
            flux_out, velocity = flux_along(beyond, d, inverse, pressure)
            speed_out = jnp.abs(velocity) + sound_speed(inverse, pressure)
            damping = 0.5 * jnp.maximum(speed_in, speed_out) + penalty * metric
            level_at = 4 * (face % 2)
            for f in range(5):
                numeric_here = 0.5 * orient_here * (flux_in[f] + flux_out[f]) + damping * (
                    inside[f] - beyond[f]
                )
                surface = orient_here * flux_in[f] - jnp.where(coupled, numeric_here, 0.0)
                lifted = gain * (surface + added_ref[face, 25 * f : 25 * f + 25, :])
                if face < 2:
                    rows = slice(25 * level_at, 25 * level_at + 25)
                    rate_ref[f, rows, :] = rate_ref[f, rows, :] + lifted
                elif face < 4:
                    for a in range(5):
                        start = 25 * a + 5 * level_at
                        rows = slice(start, start + 5)
                        rate_ref[f, rows, :] = rate_ref[f, rows, :] + lifted[5 * a : 5 * a + 5, :]
                else:
                    rows = pl.ds(level_at, 25, stride=5)
                    rate_ref[f, rows, :] = rate_ref[f, rows, :] + lifted
        return copies

    owners = []
    copies = section(0)
    for f in range(5):
        first = step_size * rate_ref[f]
        first_ref[f] = section_a2 * first
        x_ref[f] = x_ref[f] + section_b1 * first
    copies = copies + section(1)
    for f in range(5):
        register = first_ref[f] + step_size * rate_ref[f]
        out = x_ref[f] + section_b2 * register
        register_ref[f] = register[0:125]
        out_ref[f] = out[0:125]
    for copy in copies:
        copy.wait_send()


def per_device(mesh_shape, flow_state, element_level, neighbour, send_next, send_prev, coarse_face, fine_face, send_count):
    n_morton, n_sub = mesh_shape
    volume, panel, gather = (jnp.asarray(t) for t in operator_tables())
    vmem = pl.BlockSpec(memory_space=pltpu.VMEM)
    smem = pl.BlockSpec(memory_space=pltpu.SMEM)
    shape = jax.ShapeDtypeStruct(flow_state.shape, f32)
    return pl.pallas_call(
        functools.partial(kernel, n_morton, n_sub),
        out_shape=(shape, shape),
        in_specs=[vmem, vmem, vmem, smem, smem, smem, smem, smem, vmem, vmem, vmem],
        out_specs=(vmem, vmem),
        scratch_shapes=[
            pltpu.VMEM((5, 128, 128), f32),
            pltpu.VMEM((5, 128, 128), f32),
            pltpu.VMEM((5, 128, 128), f32),
            pltpu.VMEM((6, 128, 128), f32),
            pltpu.VMEM((256, 768), bf16),
            pltpu.VMEM((768, 128), f32),
            pltpu.VMEM((896, 768), bf16),
            pltpu.VMEM((16, 768), bf16),
            pltpu.VMEM((6, 128, 128), f32),
            pltpu.VMEM((6, 128, 128), f32),
            pltpu.VMEM((512, 640), bf16),
            pltpu.VMEM((512, 640), bf16),
            pltpu.VMEM((128, 128), f32),
            pltpu.VMEM((128, 128), f32),
            pltpu.VMEM((2, 2, 32, 128), f32),
            pltpu.VMEM((2, 2, 32, 128), f32),
            pltpu.VMEM((2, n_sub, 10, 128), f32),
            pltpu.VMEM((2, n_sub, 10, 128), f32),
            pltpu.SemaphoreType.DMA((2, n_sub + 2)),
            pltpu.SemaphoreType.DMA((2, n_sub + 2)),
        ],
        compiler_params=pltpu.CompilerParams(
            collective_id=0, has_side_effects=True, vmem_limit_bytes=48 * 1024 * 1024
        ),
    )(
        flow_state,
        element_level.reshape(1, -1),
        neighbour,
        send_next,
        send_prev,
        coarse_face,
        fine_face,
        send_count,
        volume,
        panel,
        gather,
    )


def solution(mesh):
    whole = ("morton", "sub")
    placed = (
        P(None, None, whole),
        P(whole),
        P(None, whole),
        P(whole, None),
        P(whole, None),
        P(whole, None, None),
        P(whole, None, None, None),
        P(whole, None),
    )
    mesh_shape = (mesh.shape["morton"], mesh.shape["sub"])
    return jax.shard_map(
        functools.partial(per_device, mesh_shape),
        mesh=mesh,
        in_specs=placed,
        out_specs=(P(None, None, whole), P(None, None, whole)),
        check_vma=False,
    )
```

time: 181 us -> 30.2 us (0.17); the launches traced: 178 us -> 29.9 us
  local copies, waits for them, and re-layouts: 79.5 us -> 6.73 us
  starting transfers between devices: 33.4 us -> 0 us
  matrix products: 32.2 us -> 0 us
  other arithmetic: 23.2 us -> 0 us
  Pallas kernels: 0 us -> 22.5 us
  waiting for transfers between devices: 6.88 us -> 0 us
  between operations: 3.11 us -> 0.67 us
    gather x22 -> x0, local copies, waits for them, and re-layouts: 32.9 us -> none  [the longest x4 12.1 us: face_terms(): outside_all = jnp.take(lookup, jnp.maximum(neighbour, 0), axis=2)]
    dot_general x36 -> x0, matrix products: 32.2 us -> none  [the longest x32 29.9 us: apply_nodes(): return jnp.einsum('fxn,fne->fxe', batched, values, precision=highest)]
    concatenate x12 -> x0, local copies, waits for them, and re-layouts: 23.3 us -> none  [the longest x4 5.49 us: rate_of(): jnp.concatenate([traces, from_prev, from_next, interpolate_panels(receive...]
    pallas_call x0 -> x1, Pallas kernels: none -> 22.5 us  [per_device(): pl.pallas_call(functools.partial(kernel, n_morton, n_sub), out_shape=(sha...]
    all_to_all x4 -> x0, starting transfers between devices: 20.8 us -> none  [the longest x2 13.1 us: rate_of(): lax.all_to_all(outgoing, 'sub', split_axis=2, concat_axis=2, tiled=True)]
    ppermute x4 -> x0, starting transfers between devices: 12.5 us -> none  [passed_along(): lax.ppermute(x, axis, [(i, (i + by) % devices) for i in range(devices)])]
    unnamed x213 -> x24, local copies, waits for them, and re-layouts: 17.2 us -> 6.73 us
    unnamed x104 -> x0, other arithmetic: 7.65 us -> none
  transfers between devices with their start and end apart: 8 -> 0, of which waited for: 3 -> 0; matrix products, arithmetic and copies ran while one was open for 17% -> 0% of each run, Pallas kernels for 0% -> 0%
where the time goes in v1:
time: 30.2 us; the launch traced here: 29.9 us
  Pallas kernels  22.5 us (75%)
  local copies, waits for them, and re-layouts  6.73 us (22%)
  between operations  0.67 us (2%)
    pallas_call x1, Pallas kernels, per_device(): pl.pallas_call(functools.partial(kernel, n_morton, n_sub), out_shape=(sha...  22.5 us
    unnamed x24, local copies, waits for them, and re-layouts  6.73 us

profile of v1, /device:TPU:0, one launch (start us, length us, event | category | flops | bytes accessed | tf_op | source)
XLA Modules:
  0.0 29.9 jit_solution(15002981470518350928)
XLA Ops:
  0.6 0.0 copy-start.9
  0.6 0.8 %copy.13.coarse_ref = s32[1,8,2]{2,1,0:T(8,128)S(1)} copy(s32[1,8,2]{1,2,0:T(2,128)} %param.16) | data formatting | bytes 128 | tf_op args[5]
  1.4 0.0 copy-done.9
  1.4 0.0 copy-start.4
  1.4 0.0 copy-start.5
  1.4 0.0 copy-start.6
  1.4 0.0 copy-start.7
  1.4 0.0 copy-start.8
  1.4 0.1 copy.14.fine_ref
  1.5 0.6 %copy-done.4 = s32[6,128]{1,0:T(8,128)S(1)} copy-done((s32[6,128]{1,0:T(8,128)S(1)}, s32[6,128]{1,0:T(8,128)}, u32[]{:S(2)}) %copy-start.4) | copy-done | bytes 3096
  2.1 0.0 copy-done.5
  2.1 0.0 copy-done.6
  2.1 0.0 copy-done.7
  2.1 0.0 copy-done.8
  2.1 0.0 copy-start
  2.1 1.0 %copy-done = f32[5,125,128]{2,1,0:T(8,128)S(1)} copy-done((f32[5,125,128]{2,1,0:T(8,128)S(1)}, f32[5,125,128]{2,1,0:T(8,128)}, u32[]{:S(2)}) %copy-start) | copy-done | bytes 320024
  3.1 0.0 copy-start.1
  3.1 0.9 %copy-done.1 = bf16[2,512,128]{2,1,0:T(8,128)(2,1)S(1)} copy-done((bf16[2,512,128]{2,1,0:T(8,128)(2,1)S(1)}, bf16[2,512,128]{2,1,0:T(8,128)(2,1)}, u32[]{:S(2)}) %copy-start.1) | copy-done | bytes 262168
  4.0 0.0 copy-start.2
  4.0 0.9 %copy-done.2 = bf16[2,128,512]{2,1,0:T(8,128)(2,1)S(1)} copy-done((bf16[2,128,512]{2,1,0:T(8,128)(2,1)S(1)}, bf16[2,128,512]{2,1,0:T(8,128)(2,1)}, u32[]{:S(2)}) %copy-start.2) | copy-done | bytes 262168
  5.0 0.0 copy-start.3
  5.0 0.9 %copy-done.3 = bf16[256,512]{1,0:T(8,128)(2,1)S(1)} copy-done((bf16[256,512]{1,0:T(8,128)(2,1)S(1)}, bf16[256,512]{1,0:T(8,128)(2,1)}, u32[]{:S(2)}) %copy-start.3) | copy-done | bytes 262168
  5.9 22.5 %shard_map.122 = (f32[5,125,128]{2,1,0:T(8,128)S(1)}, f32[5,125,128]{2,1,0:T(8,128)S(1)}) custom-call(f32[5,125,128]{2,1,0:T(8,128)S(1)} %copy-done, s32[1,128]{1,0:T(1,128)S(1)} %bitcast.1, s32[6,128]{1,0:T(8,128)S(1)} %copy-done.4, s32[1,32]{1,0:T(1,128)S(1)} %copy-done.6, s32[1,32]{1,0:T(1,128)S(1)} %copy-done.7, s32[1,8,2]{2,1,0:T(8,128)S(1)} %copy.13.coarse_ref, ...), custom_call_target="tpu_custom_call" | custom-call | tf_op jit(solution)/shard_map/pallas_call | solution.py:410
  28.5 0.7 %copy.17 = f32[5,125,128]{2,1,0:T(8,128)} copy(f32[5,125,128]{2,1,0:T(8,128)S(1)} %get-tuple-element.4) | data formatting | bytes 640000
  29.2 0.7 %copy.18 = f32[5,125,128]{2,1,0:T(8,128)} copy(f32[5,125,128]{2,1,0:T(8,128)S(1)} %get-tuple-element.5) | data formatting | bytes 640000
Async XLA Ops:
  0.6 0.8 %copy-start.9 = (s32[1,8,2,4]{1,3,2,0:T(4,128)S(1)}, s32[1,8,2,4]{1,3,2,0:T(4,128)}, u32[]{:S(2)}) copy-start(s32[1,8,2,4]{1,3,2,0:T(4,128)} %param.17) | copy-start | bytes 772
  1.4 0.7 %copy-start.4 = (s32[6,128]{1,0:T(8,128)S(1)}, s32[6,128]{1,0:T(8,128)}, u32[]{:S(2)}) copy-start(s32[6,128]{1,0:T(8,128)} %near_ref.1) | copy-start | bytes 9220
  1.4 0.7 %copy-start.5 = (s32[128]{0:T(128)S(1)}, s32[128]{0:T(128)}, u32[]{:S(2)}) copy-start(s32[128]{0:T(128)} %param.12) | copy-start | bytes 1540
  1.4 0.7 %copy-start.6 = (s32[1,32]{1,0:T(1,128)S(1)}, s32[1,32]{1,0:T(1,128)}, u32[]{:S(2)}) copy-start(s32[1,32]{1,0:T(1,128)} %next_ref.1) | copy-start | bytes 388
  1.4 0.7 %copy-start.7 = (s32[1,32]{1,0:T(1,128)S(1)}, s32[1,32]{1,0:T(1,128)}, u32[]{:S(2)}) copy-start(s32[1,32]{1,0:T(1,128)} %prev_ref.1) | copy-start | bytes 388
  1.4 0.7 %copy-start.8 = (s32[1,8]{1,0:T(1,128)S(1)}, s32[1,8]{1,0:T(1,128)}, u32[]{:S(2)}) copy-start(s32[1,8]{1,0:T(1,128)} %count_ref.1) | copy-start | bytes 100
  2.1 1.0 %copy-start = (f32[5,125,128]{2,1,0:T(8,128)S(1)}, f32[5,125,128]{2,1,0:T(8,128)}, u32[]{:S(2)}) copy-start(f32[5,125,128]{2,1,0:T(8,128)} %state_ref.1) | copy-start | bytes 960004
  3.1 0.9 %copy-start.1 = (bf16[2,512,128]{2,1,0:T(8,128)(2,1)S(1)}, bf16[2,512,128]{2,1,0:T(8,128)(2,1)}, u32[]{:S(2)}) copy-start(bf16[2,512,128]{2,1,0:T(8,128)(2,1)} %constant.8.clone.gather_ref) | copy-start | bytes 786436
  4.0 0.9 %copy-start.2 = (bf16[2,128,512]{2,1,0:T(8,128)(2,1)S(1)}, bf16[2,128,512]{2,1,0:T(8,128)(2,1)}, u32[]{:S(2)}) copy-start(bf16[2,128,512]{2,1,0:T(8,128)(2,1)} %constant.7.clone.panel_ref) | copy-start | bytes 786436
  5.0 0.9 %copy-start.3 = (bf16[256,512]{1,0:T(8,128)(2,1)S(1)}, bf16[256,512]{1,0:T(8,128)(2,1)}, u32[]{:S(2)}) copy-start(bf16[256,512]{1,0:T(8,128)(2,1)} %constant.6.clone.volume_ref) | copy-start | bytes 786436

commit v2 on v1

--- a/solution.py
+++ b/solution.py
@@ -123,6 +123,20 @@
 def kernel(
     n_morton,
     n_sub,
+    state_hbm,
+    level_hbm,
+    near_hbm,
+    next_hbm,
+    prev_hbm,
+    coarse_hbm,
+    fine_hbm,
+    count_hbm,
+    volume_hbm,
+    panel_hbm,
+    gather_hbm,
+    x_ref,
+    first_ref,
+    rate_ref,
     state_ref,
     level_ref,
     near_ref,
@@ -134,11 +148,7 @@
     volume_ref,
     panel_ref,
     gather_ref,
-    out_ref,
-    register_ref,
-    x_ref,
-    rate_ref,
-    first_ref,
+    load_sem,
     face_ref,
     face_bf_ref,
     rows_ref,
@@ -173,6 +183,29 @@
     for target in (after_id, before_id):
         pl.semaphore_signal(barrier, inc=1, device_id=target, device_id_type=MESH)
 
+    loads = [
+        pltpu.make_async_copy(source, target, load_sem.at[i])
+        for i, (source, target) in enumerate(
+            (
+                (state_hbm, state_ref),
+                (level_hbm, level_ref),
+                (fine_hbm, fine_ref),
+                (coarse_hbm, coarse_ref),
+                (next_hbm, next_ref),
+                (prev_hbm, prev_ref),
+                (near_hbm, near_ref),
+                (count_hbm, count_ref),
+                (volume_hbm, volume_ref),
+                (panel_hbm, panel_ref),
+                (gather_hbm, gather_ref),
+            )
+        )
+    ]
+    for load in loads:
+        load.start()
+    for load in loads[0:8]:
+        load.wait()
+
     level = level_ref[...]
     metric = 0.25 * jnp.left_shift(jnp.ones_like(level), level).astype(f32)
     near = near_ref[...]
@@ -213,9 +246,9 @@
             for j in range(2):
                 for q in range(4):
                     message_send[step, p, 4 * j + q : 4 * j + q + 1, :] = rows_ref[
-                        pl.ds(fine_ref[0, p, j, q], 1), :
+                        pl.ds(fine_ref[0, j, q, p], 1), :
                     ]
-                message_send[step, p, 8 + j : 9 + j, :] = rows_ref[pl.ds(coarse_ref[0, p, j], 1), :]
+                message_send[step, p, 8 + j : 9 + j, :] = rows_ref[pl.ds(coarse_ref[0, j, p], 1), :]
         for o in (4, 3, 5, 2, 6, 1, 7):
             copy = pltpu.make_async_remote_copy(
                 src_ref=message_send.at[step, peers[o]],
@@ -242,6 +275,9 @@
             copies.append(copy)
         message_recv[step, s] = message_send[step, s]
 
+        if step == 0:
+            for load in loads[8:11]:
+                load.wait()
         fields = [x_ref[f] for f in range(5)]
         inverse, pressure = gas_state(fields)
         for d in range(3):
@@ -272,7 +308,7 @@
             owner = jnp.full((16, 128), -1, jnp.int32)
             for j in range(2):
                 for p in range(n_sub):
-                    slot = jnp.where(j < count_ref[0, p], coarse_ref[0, p, j], -1)
+                    slot = jnp.where(j < count_ref[0, p], coarse_ref[0, j, p], -1)
                     owner = jnp.where(small_rows == 8 * j + p, slot, owner)
             for face in range(6):
                 spread_ref[:, 128 * face : 128 * face + 128] = jnp.where(
@@ -392,30 +428,53 @@
         first_ref[f] = section_a2 * first
         x_ref[f] = x_ref[f] + section_b1 * first
     copies = copies + section(1)
-    for f in range(5):
-        register = first_ref[f] + step_size * rate_ref[f]
-        out = x_ref[f] + section_b2 * register
-        register_ref[f] = register[0:125]
-        out_ref[f] = out[0:125]
     for copy in copies:
         copy.wait_send()
+
+
+def finish(x_ref, first_ref, rate_ref, out_hbm, register_hbm, out_ref, register_ref, sem):
+    copies = []
+    for f in range(5):
+        register = first_ref[f, 0:125, :] + step_size * rate_ref[f, 0:125, :]
+        register_ref[f] = register
+        out_ref[f] = x_ref[f, 0:125, :] + section_b2 * register
+        copies.append(pltpu.make_async_copy(register_ref.at[f], register_hbm.at[f], sem.at[0, f]))
+        copies.append(pltpu.make_async_copy(out_ref.at[f], out_hbm.at[f], sem.at[1, f]))
+        for copy in copies[-2:]:
+            copy.start()
+    for copy in copies:
+        copy.wait()
 
 
 def per_device(mesh_shape, flow_state, element_level, neighbour, send_next, send_prev, coarse_face, fine_face, send_count):
     n_morton, n_sub = mesh_shape
     volume, panel, gather = (jnp.asarray(t) for t in operator_tables())
     vmem = pl.BlockSpec(memory_space=pltpu.VMEM)
-    smem = pl.BlockSpec(memory_space=pltpu.SMEM)
+    hbm = pl.BlockSpec(memory_space=pltpu.HBM)
     shape = jax.ShapeDtypeStruct(flow_state.shape, f32)
-    return pl.pallas_call(
+    block = jax.ShapeDtypeStruct((5, 128, 128), f32)
+    operands = (
+        flow_state,
+        element_level.reshape(1, -1),
+        neighbour,
+        send_next,
+        send_prev,
+        jnp.transpose(coarse_face, (0, 2, 1)),
+        jnp.transpose(fine_face, (0, 2, 3, 1)),
+        send_count,
+        volume,
+        panel,
+        gather,
+    )
+    spaces = [pltpu.VMEM] * 3 + [pltpu.SMEM] * 5 + [pltpu.VMEM] * 3
+    pieces = pl.pallas_call(
         functools.partial(kernel, n_morton, n_sub),
-        out_shape=(shape, shape),
-        in_specs=[vmem, vmem, vmem, smem, smem, smem, smem, smem, vmem, vmem, vmem],
-        out_specs=(vmem, vmem),
-        scratch_shapes=[
-            pltpu.VMEM((5, 128, 128), f32),
-            pltpu.VMEM((5, 128, 128), f32),
-            pltpu.VMEM((5, 128, 128), f32),
+        out_shape=(block, block, block),
+        in_specs=[hbm] * len(operands),
+        out_specs=(vmem, vmem, vmem),
+        scratch_shapes=[space(x.shape, x.dtype) for space, x in zip(spaces, operands)]
+        + [
+            pltpu.SemaphoreType.DMA((len(operands),)),
             pltpu.VMEM((6, 128, 128), f32),
             pltpu.VMEM((256, 768), bf16),
             pltpu.VMEM((768, 128), f32),
@@ -435,21 +494,21 @@
             pltpu.SemaphoreType.DMA((2, n_sub + 2)),
         ],
         compiler_params=pltpu.CompilerParams(
-            collective_id=0, has_side_effects=True, vmem_limit_bytes=48 * 1024 * 1024
+            collective_id=0, has_side_effects=True, vmem_limit_bytes=40 * 1024 * 1024
         ),
-    )(
-        flow_state,
-        element_level.reshape(1, -1),
-        neighbour,
-        send_next,
-        send_prev,
-        coarse_face,
-        fine_face,
-        send_count,
-        volume,
-        panel,
-        gather,
-    )
+    )(*[pltpu.with_memory_space_constraint(x, pltpu.HBM) for x in operands])
+    return pl.pallas_call(
+        finish,
+        out_shape=(shape, shape),
+        in_specs=[vmem, vmem, vmem],
+        out_specs=(hbm, hbm),
+        scratch_shapes=[
+            pltpu.VMEM(flow_state.shape, f32),
+            pltpu.VMEM(flow_state.shape, f32),
+            pltpu.SemaphoreType.DMA((2, 5)),
+        ],
+        compiler_params=pltpu.CompilerParams(vmem_limit_bytes=16 * 1024 * 1024),
+    )(*pieces)
 
 
 def solution(mesh):

time: 30.2 us -> 23.6 us (0.78)
  local copies, waits for them, and re-layouts: 6.73 us -> 0 us
    unnamed x24 -> x0, local copies, waits for them, and re-layouts: 6.73 us -> none
    pallas_call x1 -> x2, Pallas kernels: 22.5 us -> 22.8 us  [the longest x1 21.9 us: per_device(): pl.pallas_call(functools.partial(kernel, n_morton, n_sub), out_shape=(blo...]
where the time goes in v2:
time: 23.6 us; the launch traced here: 23.5 us
  Pallas kernels  22.8 us (97%)
  between operations  0.64 us (3%)
    pallas_call x1, Pallas kernels, per_device(): pl.pallas_call(functools.partial(kernel, n_morton, n_sub), out_shape=(blo...  21.9 us
    pallas_call x1, Pallas kernels, per_device(): pl.pallas_call(finish, out_shape=(shape, shape), in_specs=[vmem, vmem, vm...  0.92 us

profile of v2, /device:TPU:0, one launch (start us, length us, event | category | flops | bytes accessed | tf_op | source)
XLA Modules:
  0.0 23.5 jit_solution(14241089348765568132)
XLA Ops:
  0.6 21.9 %shard_map.122 = (f32[5,128,128]{2,1,0:T(8,128)S(1)}, f32[5,128,128]{2,1,0:T(8,128)S(1)}, f32[5,128,128]{2,1,0:T(8,128)S(1)}) custom-call(f32[5,125,128]{2,1,0:T(8,128)} %state_hbm.1, s32[1,128]{1,0:T(1,128)} %bitcast.5, s32[6,128]{1,0:T(8,128)} %near_hbm.1, s32[1,32]{1,0:T(1,128)} %next_hbm.1, s32[1,32]{1,0:T(1,128)} %prev_hbm.1, s32[1,2,8]{2,1,0:T(2,128)} %bitcast.4, ...), custom_call_target="tpu_custom_call" | custom-call | tf_op jit(solution)/shard_map/pallas_call | solution.py:470
  22.6 0.9 %shard_map.123 = (f32[5,125,128]{2,1,0:T(8,128)}, f32[5,125,128]{2,1,0:T(8,128)}) custom-call(f32[5,128,128]{2,1,0:T(8,128)S(1)} %get-tuple-element.5.x_ref, f32[5,128,128]{2,1,0:T(8,128)S(1)} %get-tuple-element.6.first_ref, f32[5,128,128]{2,1,0:T(8,128)S(1)} %get-tuple-element.7.rate_ref), custom_call_target="tpu_custom_call" | custom-call | tf_op jit(solution)/shard_map/pallas_call | solution.py:500

commit v3 on v2

--- a/solution.py
+++ b/solution.py
@@ -82,7 +82,7 @@
             rows = slice(25 * f, 25 * f + 25)
             columns = slice(128 * q + 25 * f, 128 * q + 25 * f + 25)
             panel[rows, columns] = interpolation[q].T
-            gather[columns, rows] = projection[q].T
+            gather[columns, rows] = projection[q]
     return two_parts(volume).reshape(256, 512), two_parts(panel), two_parts(gather)
 
 
@@ -118,6 +118,33 @@
 
 def sound_speed(inverse, pressure):
     return jnp.sqrt(gamma_gas * pressure * inverse)
+
+
+def mortar_part(fields):
+    inverse, pressure = gas_state(fields)
+    return inverse, pressure, sound_speed(inverse, pressure)
+
+
+def flux_by_lane(fields, parts, along):
+    inverse, pressure, sound = parts
+    normal = jnp.where(along < 0.5, fields[1], jnp.where(along < 1.5, fields[2], fields[3]))
+    velocity = normal * inverse
+    components = [
+        normal,
+        fields[1] * velocity + jnp.where(along < 0.5, pressure, 0.0),
+        fields[2] * velocity + jnp.where((along > 0.5) & (along < 1.5), pressure, 0.0),
+        fields[3] * velocity + jnp.where(along > 1.5, pressure, 0.0),
+        (fields[4] + pressure) * velocity,
+    ]
+    return components, jnp.abs(velocity) + sound
+
+
+def face_fields(ref):
+    return [ref[25 * f : 25 * f + 25, :] for f in range(5)]
+
+
+def both_halves(x):
+    return x[0:128] + x[128:256]
 
 
 def kernel(
@@ -151,14 +178,17 @@
     load_sem,
     face_ref,
     face_bf_ref,
-    rows_ref,
     pick_ref,
     spread_ref,
+    send_pick_ref,
     outside_ref,
     added_ref,
     flux_high_ref,
     flux_low_ref,
-    mortar_ref,
+    inner_ref,
+    ring_ref,
+    known_ref,
+    arrived_ref,
     numeric_ref,
     ring_send,
     ring_recv,
@@ -178,7 +208,7 @@
     peers = [lax.rem(s + o, n_sub) for o in range(n_sub)]
 
     barrier = pltpu.get_barrier_semaphore()
-    for o in range(1, n_sub):
+    for o in (4, 3, 5, 2, 6, 1, 7):
         pl.semaphore_signal(barrier, inc=1, device_id=(m, peers[o]), device_id_type=MESH)
     for target in (after_id, before_id):
         pl.semaphore_signal(barrier, inc=1, device_id=target, device_id_type=MESH)
@@ -210,18 +240,72 @@
     metric = 0.25 * jnp.left_shift(jnp.ones_like(level), level).astype(f32)
     near = near_ref[...]
     extra = near - 832
-    panel_lane = 832 + (extra & 3) * 16 + ((extra >> 2) & 1) * 8 + (extra >> 3)
-    entry = jnp.where(near >= 832, panel_lane, near)
+    panel_lane = 768 + (extra & 3) * 16 + ((extra >> 2) & 1) * 8 + (extra >> 3)
+    entry = jnp.where(near >= 832, panel_lane, jnp.where(near >= 768, near + 64, near))
+    lane = lax.broadcasted_iota(jnp.int32, (1, 128), 1)
+    low_lanes = lane < 64
+    counts = jnp.zeros((1, 128), jnp.int32)
+    for p in range(n_sub):
+        counts = jnp.where((lane & 7) == p, count_ref[0, p], counts)
+    used = ((lane >> 3) & 1) < counts
 
     for f in range(5):
         x_ref[f, 0:125, :] = state_ref[f]
         x_ref[f, 125:128, :] = jnp.ones((3, 128), f32)
-    row_ids = lax.broadcasted_iota(jnp.int32, (128, 128), 0)
     for face in range(6):
         face_ref[face, 125:126, :] = jnp.full((1, 128), float(face // 2), f32)
         face_ref[face, 126:127, :] = metric
         face_ref[face, 127:128, :] = jnp.full((1, 128), 1.0 if face % 2 else -1.0, f32)
     numeric_ref[125:128, :] = jnp.zeros((3, 128), f32)
+
+    rows = lax.broadcasted_iota(jnp.int32, (16, 128), 0)
+    lanes = lax.broadcasted_iota(jnp.int32, (16, 128), 1)
+
+    def marks(slots, target_ref, at):
+        column = jnp.full((16, 128), -1, jnp.int32)
+        for r, slot in enumerate(slots):
+            column = jnp.where(rows == r, slot, column)
+        for face in range(6):
+            hit = jnp.where(column == lanes + 128 * face, 1.0, 0.0).astype(bf16)
+            for row in at:
+                target_ref[row : row + 16, 128 * face : 128 * face + 128] = hit
+
+    for b in range(4):
+        list_ref = (next_ref, prev_ref)[b // 2]
+        marks([list_ref[0, 16 * (b % 2) + i] for i in range(16)], send_pick_ref, [16 * b])
+    for p in range(n_sub):
+        marks(
+            [fine_ref[0, r // 4, r % 4, p] for r in range(8)] + [coarse_ref[0, j, p] for j in range(2)],
+            send_pick_ref,
+            [64 + 16 * p],
+        )
+
+    def onto_planes(target_ref, face, f, value):
+        level_at = 4 * (face % 2)
+        if face < 2:
+            plane = slice(25 * level_at, 25 * level_at + 25)
+            target_ref[f, plane, :] = target_ref[f, plane, :] + value
+        elif face < 4:
+            for a in range(5):
+                start = 25 * a + 5 * level_at
+                plane = slice(start, start + 5)
+                target_ref[f, plane, :] = target_ref[f, plane, :] + value[5 * a : 5 * a + 5, :]
+        else:
+            plane = pl.ds(level_at, 25, stride=5)
+            target_ref[f, plane, :] = target_ref[f, plane, :] + value
+
+    def store_added(product):
+        added = both_halves(product)
+        for face in range(6):
+            added_ref[face] = added[:, 128 * face : 128 * face + 128]
+
+    def panels_of(source):
+        coarse_rows = jnp.concatenate([source[:, 8 + j, :] for j in range(2)], axis=0)
+        high, low = split(coarse_rows)
+        wide = dot(high, panel_ref[0]) + dot(low, panel_ref[0]) + dot(high, panel_ref[1])
+        return [wide[:, 128 * q : 128 * q + 128] for q in range(4)]
+
+    gain = lift_gain * metric
 
     def section(step):
         for face in range(6):
@@ -237,18 +321,21 @@
                 else:
                     face_ref[face, base : base + 25, :] = x_ref[f, pl.ds(level_at, 25, stride=5), :]
         for face in range(6):
-            rows_ref[128 * face : 128 * face + 128, :] = face_ref[face].T
-
+            high, low = split(face_ref[face])
+            face_bf_ref[0:128, 128 * face : 128 * face + 128] = high
+            face_bf_ref[128:256, 128 * face : 128 * face + 128] = low
+        across = (((1,), (1,)), ((), ()))
+        packed = lax.dot_general(
+            send_pick_ref[...], face_bf_ref[...], across, preferred_element_type=f32
+        )
+        packed = packed[:, 0:128] + packed[:, 128:256]
+        for p in range(n_sub):
+            message_send[step, p] = packed[64 + 16 * p : 74 + 16 * p, :]
+        for side in range(2):
+            ring_send[step, side] = packed[32 * side : 32 * side + 32, :]
         if step == 0:
             pl.semaphore_wait(barrier, n_sub + 1)
-        copies = []
-        for p in range(n_sub):
-            for j in range(2):
-                for q in range(4):
-                    message_send[step, p, 4 * j + q : 4 * j + q + 1, :] = rows_ref[
-                        pl.ds(fine_ref[0, j, q, p], 1), :
-                    ]
-                message_send[step, p, 8 + j : 9 + j, :] = rows_ref[pl.ds(coarse_ref[0, j, p], 1), :]
+        messages = []
         for o in (4, 3, 5, 2, 6, 1, 7):
             copy = pltpu.make_async_remote_copy(
                 src_ref=message_send.at[step, peers[o]],
@@ -259,10 +346,9 @@
                 device_id_type=MESH,
             )
             copy.start()
-            copies.append(copy)
-        for side, (list_ref, target) in enumerate(((next_ref, after_id), (prev_ref, before_id))):
-            for i in range(32):
-                ring_send[step, side, i : i + 1, :] = rows_ref[pl.ds(list_ref[0, i], 1), :]
+            messages.append(copy)
+        rings = []
+        for side, target in enumerate((after_id, before_id)):
             copy = pltpu.make_async_remote_copy(
                 src_ref=ring_send.at[step, side],
                 dst_ref=ring_recv.at[step, side],
@@ -272,12 +358,18 @@
                 device_id_type=MESH,
             )
             copy.start()
-            copies.append(copy)
+            rings.append(copy)
         message_recv[step, s] = message_send[step, s]
 
         if step == 0:
             for load in loads[8:11]:
                 load.wait()
+        else:
+            for face in range(6):
+                for f in range(5):
+                    onto_planes(rate_ref, face, f, gain * added_ref[face, 25 * f : 25 * f + 25, :])
+            for f in range(5):
+                first_ref[f] = (section_a2 * step_size) * rate_ref[f]
         fields = [x_ref[f] for f in range(5)]
         inverse, pressure = gas_state(fields)
         for d in range(3):
@@ -290,110 +382,56 @@
             high, low = split(viscosity * metric * fields[f])
             flux_high_ref[384:512, 128 * f : 128 * f + 128] = high
             flux_low_ref[384:512, 128 * f : 128 * f + 128] = low
-        both = dot(volume_ref[...], flux_high_ref[...])
-        total = both[0:128] + both[128:256] + dot(volume_ref[0:128, :], flux_low_ref[...])
+        total = both_halves(dot(volume_ref[...], flux_high_ref[...]))
+        total = total + dot(volume_ref[0:128, :], flux_low_ref[...])
         for f in range(5):
             rate_ref[f] = metric * total[:, 128 * f : 128 * f + 128]
 
         if step == 0:
             for face in range(6):
                 wanted = entry[face : face + 1, :]
-                for block in range(7):
-                    hit = (row_ids + 128 * block) == wanted
-                    pick_ref[128 * block : 128 * block + 128, 128 * face : 128 * face + 128] = jnp.where(
-                        hit, 1.0, 0.0
+                for block in range(56):
+                    pick_ref[16 * block : 16 * block + 16, 128 * face : 128 * face + 128] = jnp.where(
+                        rows + 16 * block == wanted, 1.0, 0.0
                     ).astype(bf16)
-            small_rows = lax.broadcasted_iota(jnp.int32, (16, 128), 0)
-            small_lanes = lax.broadcasted_iota(jnp.int32, (16, 128), 1)
-            owner = jnp.full((16, 128), -1, jnp.int32)
-            for j in range(2):
-                for p in range(n_sub):
-                    slot = jnp.where(j < count_ref[0, p], coarse_ref[0, j, p], -1)
-                    owner = jnp.where(small_rows == 8 * j + p, slot, owner)
-            for face in range(6):
-                spread_ref[:, 128 * face : 128 * face + 128] = jnp.where(
-                    owner == small_lanes + 128 * face, 1.0, 0.0
-                ).astype(bf16)
-            owners.append(owner)
-        for face in range(6):
-            high, low = split(face_ref[face])
-            face_bf_ref[0:128, 128 * face : 128 * face + 128] = high
-            face_bf_ref[128:256, 128 * face : 128 * face + 128] = low
-        local = dot(face_bf_ref[...], pick_ref[0:768, :])
-        local = local[0:128] + local[128:256]
+            spread_ref[0:64, :] = pick_ref[768:832, :]
+            owned = [
+                jnp.where(j < count_ref[0, p], coarse_ref[0, j, p], -1) for j in range(2) for p in range(n_sub)
+            ]
+            marks(owned, spread_ref, [64, 80, 96, 112])
+        local = both_halves(dot(face_bf_ref[...], pick_ref[0:768, :]))
         for face in range(6):
             outside_ref[face] = local[:, 128 * face : 128 * face + 128]
-
-        def panels_of(source):
-            coarse_rows = jnp.concatenate(
-                [source[step, :, 8 + j, :] for j in range(2)], axis=0
-            )
-            high, low = split(coarse_rows)
-            wide = dot(high, panel_ref[0]) + dot(low, panel_ref[0]) + dot(high, panel_ref[1])
-            return [wide[:, 128 * q : 128 * q + 128] for q in range(4)]
-
-        own_panels = panels_of(message_send)
-
-        for copy in copies:
+        inner_ref[...] = both_halves(
+            lax.dot_general(face_bf_ref[...], pick_ref[768:896, :], across, preferred_element_type=f32)
+        )
+        own = jnp.concatenate([jnp.zeros((64, 128), f32)] + panels_of(message_send.at[step]), axis=0).T
+        known_ref[...] = jnp.where(low_lanes, inner_ref[...], own)
+        inner_facts = [inner_ref[125 + i : 126 + i, :] for i in range(3)]
+
+        for copy in rings:
             copy.wait_recv()
-
-        arrived = jnp.concatenate(
-            [ring_recv[step, 0], ring_recv[step, 1]] + panels_of(message_recv), axis=0
+        ring_ref[...] = jnp.concatenate(
+            [jnp.zeros((64, 128), f32), ring_recv[step, 0], ring_recv[step, 1]], axis=0
         ).T
-        high, low = split(arrived)
-        remote = dot(jnp.concatenate([high, low], axis=0), pick_ref[768:896, :])
-        remote = remote[0:128] + remote[128:256]
-        for face in range(6):
-            outside_ref[face] = outside_ref[face] + remote[:, 128 * face : 128 * face + 128]
-
-        fine_rows = [
-            message_recv[step, :, 4 * j + q, :] for q in range(4) for j in range(2)
-        ]
-        mortar_ref[...] = jnp.concatenate(fine_rows + own_panels, axis=0).T
-        left = lax.broadcasted_iota(jnp.int32, (1, 128), 1) < 64
-
-        def across(x):
-            return pltpu.roll(x, 64, 1)
-
-        facts = [mortar_ref[125 + i : 126 + i, :] for i in range(3)]
-        facts = [jnp.where(left, x, across(x)) for x in facts]
-        along, mortar_metric, orient = facts
-        sides = [mortar_ref[25 * f : 25 * f + 25, :] for f in range(5)]
-        inverse, pressure = gas_state(sides)
-        normal = jnp.where(along < 0.5, sides[1], jnp.where(along < 1.5, sides[2], sides[3]))
-        velocity = normal * inverse
-        speed = jnp.abs(velocity) + sound_speed(inverse, pressure)
-        components = [
-            normal,
-            sides[1] * velocity + jnp.where(along < 0.5, pressure, 0.0),
-            sides[2] * velocity + jnp.where((along > 0.5) & (along < 1.5), pressure, 0.0),
-            sides[3] * velocity + jnp.where(along > 1.5, pressure, 0.0),
-            (sides[4] + pressure) * velocity,
-        ]
-        damping = 0.5 * jnp.maximum(speed, across(speed)) + penalty * mortar_metric
+        along, scale, orient = inner_facts
+        inside = face_fields(inner_ref)
+        beyond = face_fields(ring_ref)
+        flux_in, speed_in = flux_by_lane(inside, mortar_part(inside), along)
+        flux_out, speed_out = flux_by_lane(beyond, mortar_part(beyond), along)
+        damping = 0.5 * jnp.maximum(speed_in, speed_out) + penalty * scale
         for f in range(5):
-            numeric_ref[25 * f : 25 * f + 25, :] = 0.5 * orient * (
-                components[f] + across(components[f])
-            ) + damping * (sides[f] - across(sides[f]))
-        numeric = numeric_ref[...].T
-        wide = jnp.concatenate([numeric[16 * q : 16 * q + 16, :] for q in range(4)], axis=1)
-        high, low = split(wide)
-        projected = dot(high, gather_ref[0]) + dot(low, gather_ref[0]) + dot(high, gather_ref[1])
-        projected = jnp.where(owners[0] >= 0, projected, 0.0).T
-        high, low = split(projected)
-        added = dot(jnp.concatenate([high, low], axis=0), spread_ref[...])
-        added = added[0:128] + added[128:256]
-        for face in range(6):
-            added_ref[face] = added[:, 128 * face : 128 * face + 128]
-
-        gain = lift_gain * metric
+            value = 0.5 * orient * (flux_in[f] + flux_out[f]) + damping * (inside[f] - beyond[f])
+            numeric_ref[25 * f : 25 * f + 25, :] = jnp.where(low_lanes, 0.0, -value)
+        high, low = split(numeric_ref[...])
+        store_added(dot(jnp.concatenate([high, low], axis=0), pick_ref[768:896, :]))
+
         for face in range(6):
             d = face // 2
             orient_here = 1.0 if face % 2 else -1.0
-            inside = [face_ref[face, 25 * f : 25 * f + 25, :] for f in range(5)]
-            beyond = [outside_ref[face, 25 * f : 25 * f + 25, :] for f in range(5)]
-            coupled = near[face : face + 1, :] >= 0
-            beyond = [jnp.where(coupled, b, i) for b, i in zip(beyond, inside)]
+            inside = face_fields(face_ref.at[face])
+            beyond = face_fields(outside_ref.at[face])
+            coupled = (near[face : face + 1, :] >= 0) & (near[face : face + 1, :] < 768)
             inverse, pressure = gas_state(inside)
             flux_in, velocity = flux_along(inside, d, inverse, pressure)
             speed_in = jnp.abs(velocity) + sound_speed(inverse, pressure)
@@ -401,32 +439,56 @@
             flux_out, velocity = flux_along(beyond, d, inverse, pressure)
             speed_out = jnp.abs(velocity) + sound_speed(inverse, pressure)
             damping = 0.5 * jnp.maximum(speed_in, speed_out) + penalty * metric
-            level_at = 4 * (face % 2)
             for f in range(5):
-                numeric_here = 0.5 * orient_here * (flux_in[f] + flux_out[f]) + damping * (
-                    inside[f] - beyond[f]
-                )
-                surface = orient_here * flux_in[f] - jnp.where(coupled, numeric_here, 0.0)
-                lifted = gain * (surface + added_ref[face, 25 * f : 25 * f + 25, :])
-                if face < 2:
-                    rows = slice(25 * level_at, 25 * level_at + 25)
-                    rate_ref[f, rows, :] = rate_ref[f, rows, :] + lifted
-                elif face < 4:
-                    for a in range(5):
-                        start = 25 * a + 5 * level_at
-                        rows = slice(start, start + 5)
-                        rate_ref[f, rows, :] = rate_ref[f, rows, :] + lifted[5 * a : 5 * a + 5, :]
-                else:
-                    rows = pl.ds(level_at, 25, stride=5)
-                    rate_ref[f, rows, :] = rate_ref[f, rows, :] + lifted
-        return copies
-
-    owners = []
+                value = 0.5 * orient_here * (flux_in[f] + flux_out[f]) + damping * (inside[f] - beyond[f])
+                surface = orient_here * flux_in[f] - jnp.where(coupled, value, 0.0)
+                surface = surface + added_ref[face, 25 * f : 25 * f + 25, :]
+                onto_planes(rate_ref, face, f, gain * surface)
+        if step == 0:
+            for f in range(5):
+                x_ref[f] = x_ref[f] + (section_b1 * step_size) * rate_ref[f]
+
+        known = face_fields(known_ref)
+        known_parts = mortar_part(known)
+        for copy in messages:
+            copy.wait_recv()
+        fine_rows = [message_recv[step, :, 4 * j + q, :] for q in range(4) for j in range(2)]
+        arrived_ref[...] = jnp.concatenate(panels_of(message_recv.at[step]) + fine_rows, axis=0).T
+        facts = [
+            jnp.where(low_lanes, x, arrived_ref[125 + i : 126 + i, :]) for i, x in enumerate(inner_facts)
+        ]
+        along, scale, orient = facts
+        valid = jnp.where(low_lanes, orient, jnp.where(used, 1.0, 0.0)) != 0.0
+        arrived = face_fields(arrived_ref)
+        flux_new, speed_new = flux_by_lane(arrived, mortar_part(arrived), along)
+        flux_old, speed_old = flux_by_lane(known, known_parts, along)
+        damping = 0.5 * jnp.maximum(speed_new, speed_old) + penalty * scale
+        damping = jnp.where(low_lanes, -damping, damping)
+        for f in range(5):
+            value = 0.5 * orient * (flux_new[f] + flux_old[f]) + damping * (arrived[f] - known[f])
+            numeric_ref[25 * f : 25 * f + 25, :] = value
+        numeric = numeric_ref[...]
+        high, low = split(numeric)
+        wide = dot(gather_ref[0], high) + dot(gather_ref[0], low) + dot(gather_ref[1], high)
+        ready = -numeric
+        for q in range(4):
+            block = (lane >= 64 + 16 * q) & (lane < 80 + 16 * q)
+            ready = jnp.where(block, wide[128 * q : 128 * q + 128, :], ready)
+        ready = jnp.where(valid, ready, 0.0)
+        high, low = split(ready)
+        store_added(dot(jnp.concatenate([high, low], axis=0), spread_ref[...]))
+        if step == 0:
+            gain_now = (section_b1 * step_size * lift_gain) * metric
+            for face in range(6):
+                for f in range(5):
+                    onto_planes(x_ref, face, f, gain_now * added_ref[face, 25 * f : 25 * f + 25, :])
+        else:
+            for face in range(6):
+                for f in range(5):
+                    onto_planes(rate_ref, face, f, gain * added_ref[face, 25 * f : 25 * f + 25, :])
+        return rings + messages
+
     copies = section(0)
-    for f in range(5):
-        first = step_size * rate_ref[f]
-        first_ref[f] = section_a2 * first
-        x_ref[f] = x_ref[f] + section_b1 * first
     copies = copies + section(1)
     for copy in copies:
         copy.wait_send()
@@ -477,13 +539,16 @@
             pltpu.SemaphoreType.DMA((len(operands),)),
             pltpu.VMEM((6, 128, 128), f32),
             pltpu.VMEM((256, 768), bf16),
-            pltpu.VMEM((768, 128), f32),
             pltpu.VMEM((896, 768), bf16),
-            pltpu.VMEM((16, 768), bf16),
+            pltpu.VMEM((128, 768), bf16),
+            pltpu.VMEM((192, 768), bf16),
             pltpu.VMEM((6, 128, 128), f32),
             pltpu.VMEM((6, 128, 128), f32),
             pltpu.VMEM((512, 640), bf16),
             pltpu.VMEM((512, 640), bf16),
+            pltpu.VMEM((128, 128), f32),
+            pltpu.VMEM((128, 128), f32),
+            pltpu.VMEM((128, 128), f32),
             pltpu.VMEM((128, 128), f32),
             pltpu.VMEM((128, 128), f32),
             pltpu.VMEM((2, 2, 32, 128), f32),

time: 23.6 us -> 24.8 us (1.051)
  Pallas kernels: 22.8 us -> 24.1 us
    pallas_call x1, Pallas kernels: 21.9 us -> 23.1 us  [per_device(): pl.pallas_call(functools.partial(kernel, n_morton, n_sub), out_shape=(blo...]
where the time goes in v3:
time: 24.8 us; the launch traced here: 24.7 us
  Pallas kernels  24.1 us (97%)
  between operations  0.64 us (3%)
    pallas_call x1, Pallas kernels, per_device(): pl.pallas_call(functools.partial(kernel, n_morton, n_sub), out_shape=(blo...  23.1 us
    pallas_call x1, Pallas kernels, per_device(): pl.pallas_call(finish, out_shape=(shape, shape), in_specs=[vmem, vmem, vm...  0.92 us

profile of v3, /device:TPU:0, one launch (start us, length us, event | category | flops | bytes accessed | tf_op | source)
XLA Modules:
  0.0 24.7 jit_solution(14029104423462727034)
XLA Ops:
  0.6 23.1 %shard_map.122 = (f32[5,128,128]{2,1,0:T(8,128)S(1)}, f32[5,128,128]{2,1,0:T(8,128)S(1)}, f32[5,128,128]{2,1,0:T(8,128)S(1)}) custom-call(f32[5,125,128]{2,1,0:T(8,128)} %state_hbm.1, s32[1,128]{1,0:T(1,128)} %bitcast.5, s32[6,128]{1,0:T(8,128)} %near_hbm.1, s32[1,32]{1,0:T(1,128)} %next_hbm.1, s32[1,32]{1,0:T(1,128)} %prev_hbm.1, s32[1,2,8]{2,1,0:T(2,128)} %bitcast.4, ...), custom_call_target="tpu_custom_call" | custom-call | tf_op jit(solution)/shard_map/pallas_call | solution.py:532
  23.8 0.9 %shard_map.123 = (f32[5,125,128]{2,1,0:T(8,128)}, f32[5,125,128]{2,1,0:T(8,128)}) custom-call(f32[5,128,128]{2,1,0:T(8,128)S(1)} %get-tuple-element.5.x_ref, f32[5,128,128]{2,1,0:T(8,128)S(1)} %get-tuple-element.6.first_ref, f32[5,128,128]{2,1,0:T(8,128)S(1)} %get-tuple-element.7.rate_ref), custom_call_target="tpu_custom_call" | custom-call | tf_op jit(solution)/shard_map/pallas_call | solution.py:565

commit v4 on v3

--- a/solution.py
+++ b/solution.py
@@ -190,6 +190,7 @@
     known_ref,
     arrived_ref,
     numeric_ref,
+    passed_ref,
     ring_send,
     ring_recv,
     message_send,
@@ -257,6 +258,7 @@
         face_ref[face, 126:127, :] = metric
         face_ref[face, 127:128, :] = jnp.full((1, 128), 1.0 if face % 2 else -1.0, f32)
     numeric_ref[125:128, :] = jnp.zeros((3, 128), f32)
+    passed_ref[125:128, :] = jnp.zeros((3, 128), f32)
 
     rows = lax.broadcasted_iota(jnp.int32, (16, 128), 0)
     lanes = lax.broadcasted_iota(jnp.int32, (16, 128), 1)
@@ -335,6 +337,18 @@
             ring_send[step, side] = packed[32 * side : 32 * side + 32, :]
         if step == 0:
             pl.semaphore_wait(barrier, n_sub + 1)
+        rings = []
+        for side, target in enumerate((after_id, before_id)):
+            copy = pltpu.make_async_remote_copy(
+                src_ref=ring_send.at[step, side],
+                dst_ref=ring_recv.at[step, side],
+                send_sem=send_sem.at[step, n_sub + side],
+                recv_sem=recv_sem.at[step, n_sub + side],
+                device_id=target,
+                device_id_type=MESH,
+            )
+            copy.start()
+            rings.append(copy)
         messages = []
         for o in (4, 3, 5, 2, 6, 1, 7):
             copy = pltpu.make_async_remote_copy(
@@ -347,18 +361,6 @@
             )
             copy.start()
             messages.append(copy)
-        rings = []
-        for side, target in enumerate((after_id, before_id)):
-            copy = pltpu.make_async_remote_copy(
-                src_ref=ring_send.at[step, side],
-                dst_ref=ring_recv.at[step, side],
-                send_sem=send_sem.at[step, n_sub + side],
-                recv_sem=recv_sem.at[step, n_sub + side],
-                device_id=target,
-                device_id_type=MESH,
-            )
-            copy.start()
-            rings.append(copy)
         message_recv[step, s] = message_send[step, s]
 
         if step == 0:
@@ -395,6 +397,7 @@
                         rows + 16 * block == wanted, 1.0, 0.0
                     ).astype(bf16)
             spread_ref[0:64, :] = pick_ref[768:832, :]
+            spread_ref[128:256, :] = pick_ref[768:896, :]
             owned = [
                 jnp.where(j < count_ref[0, p], coarse_ref[0, j, p], -1) for j in range(2) for p in range(n_sub)
             ]
@@ -408,23 +411,6 @@
         own = jnp.concatenate([jnp.zeros((64, 128), f32)] + panels_of(message_send.at[step]), axis=0).T
         known_ref[...] = jnp.where(low_lanes, inner_ref[...], own)
         inner_facts = [inner_ref[125 + i : 126 + i, :] for i in range(3)]
-
-        for copy in rings:
-            copy.wait_recv()
-        ring_ref[...] = jnp.concatenate(
-            [jnp.zeros((64, 128), f32), ring_recv[step, 0], ring_recv[step, 1]], axis=0
-        ).T
-        along, scale, orient = inner_facts
-        inside = face_fields(inner_ref)
-        beyond = face_fields(ring_ref)
-        flux_in, speed_in = flux_by_lane(inside, mortar_part(inside), along)
-        flux_out, speed_out = flux_by_lane(beyond, mortar_part(beyond), along)
-        damping = 0.5 * jnp.maximum(speed_in, speed_out) + penalty * scale
-        for f in range(5):
-            value = 0.5 * orient * (flux_in[f] + flux_out[f]) + damping * (inside[f] - beyond[f])
-            numeric_ref[25 * f : 25 * f + 25, :] = jnp.where(low_lanes, 0.0, -value)
-        high, low = split(numeric_ref[...])
-        store_added(dot(jnp.concatenate([high, low], axis=0), pick_ref[768:896, :]))
 
         for face in range(6):
             d = face // 2
@@ -442,7 +428,6 @@
             for f in range(5):
                 value = 0.5 * orient_here * (flux_in[f] + flux_out[f]) + damping * (inside[f] - beyond[f])
                 surface = orient_here * flux_in[f] - jnp.where(coupled, value, 0.0)
-                surface = surface + added_ref[face, 25 * f : 25 * f + 25, :]
                 onto_planes(rate_ref, face, f, gain * surface)
         if step == 0:
             for f in range(5):
@@ -450,10 +435,16 @@
 
         known = face_fields(known_ref)
         known_parts = mortar_part(known)
-        for copy in messages:
+        inside = face_fields(inner_ref)
+        flux_in, speed_in = flux_by_lane(inside, mortar_part(inside), inner_facts[0])
+        for copy in rings + messages:
             copy.wait_recv()
+        panels = panels_of(message_recv.at[step])
+        ring_ref[...] = jnp.concatenate(
+            [jnp.zeros((64, 128), f32), ring_recv[step, 0], ring_recv[step, 1]], axis=0
+        ).T
         fine_rows = [message_recv[step, :, 4 * j + q, :] for q in range(4) for j in range(2)]
-        arrived_ref[...] = jnp.concatenate(panels_of(message_recv.at[step]) + fine_rows, axis=0).T
+        arrived_ref[...] = jnp.concatenate(panels + fine_rows, axis=0).T
         facts = [
             jnp.where(low_lanes, x, arrived_ref[125 + i : 126 + i, :]) for i, x in enumerate(inner_facts)
         ]
@@ -470,12 +461,19 @@
         numeric = numeric_ref[...]
         high, low = split(numeric)
         wide = dot(gather_ref[0], high) + dot(gather_ref[0], low) + dot(gather_ref[1], high)
+        beyond = face_fields(ring_ref)
+        along, scale, orient = inner_facts
+        flux_out, speed_out = flux_by_lane(beyond, mortar_part(beyond), along)
+        damping = 0.5 * jnp.maximum(speed_in, speed_out) + penalty * scale
+        for f in range(5):
+            value = 0.5 * orient * (flux_in[f] + flux_out[f]) + damping * (inside[f] - beyond[f])
+            passed_ref[25 * f : 25 * f + 25, :] = jnp.where(low_lanes, 0.0, -value)
         ready = -numeric
         for q in range(4):
             block = (lane >= 64 + 16 * q) & (lane < 80 + 16 * q)
             ready = jnp.where(block, wide[128 * q : 128 * q + 128, :], ready)
         ready = jnp.where(valid, ready, 0.0)
-        high, low = split(ready)
+        high, low = split(jnp.concatenate([ready, passed_ref[...]], axis=1))
         store_added(dot(jnp.concatenate([high, low], axis=0), spread_ref[...]))
         if step == 0:
             gain_now = (section_b1 * step_size * lift_gain) * metric
@@ -540,12 +538,13 @@
             pltpu.VMEM((6, 128, 128), f32),
             pltpu.VMEM((256, 768), bf16),
             pltpu.VMEM((896, 768), bf16),
-            pltpu.VMEM((128, 768), bf16),
+            pltpu.VMEM((256, 768), bf16),
             pltpu.VMEM((192, 768), bf16),
             pltpu.VMEM((6, 128, 128), f32),
             pltpu.VMEM((6, 128, 128), f32),
             pltpu.VMEM((512, 640), bf16),
             pltpu.VMEM((512, 640), bf16),
+            pltpu.VMEM((128, 128), f32),
             pltpu.VMEM((128, 128), f32),
             pltpu.VMEM((128, 128), f32),
             pltpu.VMEM((128, 128), f32),

time: 24.8 us -> 23.2 us (0.935)
  Pallas kernels: 24.1 us -> 22.4 us
    pallas_call x1, Pallas kernels: 23.1 us -> 21.5 us  [per_device(): pl.pallas_call(functools.partial(kernel, n_morton, n_sub), out_shape=(blo...]
where the time goes in v4:
time: 23.2 us; the launch traced here: 23.1 us
  Pallas kernels  22.4 us (97%)
  between operations  0.64 us (3%)
    pallas_call x1, Pallas kernels, per_device(): pl.pallas_call(functools.partial(kernel, n_morton, n_sub), out_shape=(blo...  21.5 us
    pallas_call x1, Pallas kernels, per_device(): pl.pallas_call(finish, out_shape=(shape, shape), in_specs=[vmem, vmem, vm...  0.92 us

profile of v4, /device:TPU:0, one launch (start us, length us, event | category | flops | bytes accessed | tf_op | source)
XLA Modules:
  0.0 23.1 jit_solution(9905841527427116928)
XLA Ops:
  0.6 21.5 %shard_map.122 = (f32[5,128,128]{2,1,0:T(8,128)S(1)}, f32[5,128,128]{2,1,0:T(8,128)S(1)}, f32[5,128,128]{2,1,0:T(8,128)S(1)}) custom-call(f32[5,125,128]{2,1,0:T(8,128)} %state_hbm.1, s32[1,128]{1,0:T(1,128)} %bitcast.5, s32[6,128]{1,0:T(8,128)} %near_hbm.1, s32[1,32]{1,0:T(1,128)} %next_hbm.1, s32[1,32]{1,0:T(1,128)} %prev_hbm.1, s32[1,2,8]{2,1,0:T(2,128)} %bitcast.4, ...), custom_call_target="tpu_custom_call" | custom-call | tf_op jit(solution)/shard_map/pallas_call | solution.py:530
  22.2 0.9 %shard_map.123 = (f32[5,125,128]{2,1,0:T(8,128)}, f32[5,125,128]{2,1,0:T(8,128)}) custom-call(f32[5,128,128]{2,1,0:T(8,128)S(1)} %get-tuple-element.5.x_ref, f32[5,128,128]{2,1,0:T(8,128)S(1)} %get-tuple-element.6.first_ref, f32[5,128,128]{2,1,0:T(8,128)S(1)} %get-tuple-element.7.rate_ref), custom_call_target="tpu_custom_call" | custom-call | tf_op jit(solution)/shard_map/pallas_call | solution.py:564

commit v5 on v4

--- a/solution.py
+++ b/solution.py
@@ -83,7 +83,8 @@
             columns = slice(128 * q + 25 * f, 128 * q + 25 * f + 25)
             panel[rows, columns] = interpolation[q].T
             gather[columns, rows] = projection[q]
-    return two_parts(volume).reshape(256, 512), two_parts(panel), two_parts(gather)
+    beside = two_parts(gather).reshape(8, 128, 128).transpose(1, 0, 2).reshape(128, 1024)
+    return two_parts(volume).reshape(256, 512), two_parts(panel).reshape(256, 512), beside
 
 
 def split(x):
@@ -304,7 +305,10 @@
     def panels_of(source):
         coarse_rows = jnp.concatenate([source[:, 8 + j, :] for j in range(2)], axis=0)
         high, low = split(coarse_rows)
-        wide = dot(high, panel_ref[0]) + dot(low, panel_ref[0]) + dot(high, panel_ref[1])
+        upper = jnp.concatenate([high, high], axis=1)
+        lower = jnp.concatenate([low, jnp.zeros_like(low)], axis=1)
+        wide = dot(jnp.concatenate([upper, lower], axis=0), panel_ref[...])
+        wide = wide[0:16] + wide[16:32]
         return [wide[:, 128 * q : 128 * q + 128] for q in range(4)]
 
     gain = lift_gain * metric
@@ -337,6 +341,18 @@
             ring_send[step, side] = packed[32 * side : 32 * side + 32, :]
         if step == 0:
             pl.semaphore_wait(barrier, n_sub + 1)
+        messages = []
+        for o in (4,):
+            copy = pltpu.make_async_remote_copy(
+                src_ref=message_send.at[step, peers[o]],
+                dst_ref=message_recv.at[step, s],
+                send_sem=send_sem.at[step, o],
+                recv_sem=recv_sem.at[step, o],
+                device_id=(m, peers[o]),
+                device_id_type=MESH,
+            )
+            copy.start()
+            messages.append(copy)
         rings = []
         for side, target in enumerate((after_id, before_id)):
             copy = pltpu.make_async_remote_copy(
@@ -349,8 +365,7 @@
             )
             copy.start()
             rings.append(copy)
-        messages = []
-        for o in (4, 3, 5, 2, 6, 1, 7):
+        for o in (3, 5, 2, 6, 1, 7):
             copy = pltpu.make_async_remote_copy(
                 src_ref=message_send.at[step, peers[o]],
                 dst_ref=message_recv.at[step, s],
@@ -459,8 +474,12 @@
             value = 0.5 * orient * (flux_new[f] + flux_old[f]) + damping * (arrived[f] - known[f])
             numeric_ref[25 * f : 25 * f + 25, :] = value
         numeric = numeric_ref[...]
-        high, low = split(numeric)
-        wide = dot(gather_ref[0], high) + dot(gather_ref[0], low) + dot(gather_ref[1], high)
+        high = numeric.astype(bf16).astype(f32)
+        mixed = jnp.where(low_lanes, pltpu.roll(numeric - high, 64, 1), high)
+        panel_of = jnp.where(low_lanes, lane, lane - 64) >> 4
+        parts = [jnp.where(panel_of == q, mixed, 0.0) for q in range(4)]
+        parts = parts + [jnp.where((panel_of == q) & ~low_lanes, high, 0.0) for q in range(4)]
+        chosen = dot(gather_ref[...], jnp.concatenate(parts, axis=0).astype(bf16))
         beyond = face_fields(ring_ref)
         along, scale, orient = inner_facts
         flux_out, speed_out = flux_by_lane(beyond, mortar_part(beyond), along)
@@ -468,10 +487,7 @@
         for f in range(5):
             value = 0.5 * orient * (flux_in[f] + flux_out[f]) + damping * (inside[f] - beyond[f])
             passed_ref[25 * f : 25 * f + 25, :] = jnp.where(low_lanes, 0.0, -value)
-        ready = -numeric
-        for q in range(4):
-            block = (lane >= 64 + 16 * q) & (lane < 80 + 16 * q)
-            ready = jnp.where(block, wide[128 * q : 128 * q + 128, :], ready)
+        ready = jnp.where(low_lanes, -numeric, chosen + pltpu.roll(chosen, 64, 1))
         ready = jnp.where(valid, ready, 0.0)
         high, low = split(jnp.concatenate([ready, passed_ref[...]], axis=1))
         store_added(dot(jnp.concatenate([high, low], axis=0), spread_ref[...]))

time: 23.2 us -> 23 us (level)
  no operation moved by 1% of the time
where the time goes in v5:
time: 23 us; the launch traced here: 22.9 us
  Pallas kernels  22.3 us (97%)
  between operations  0.64 us (3%)
    pallas_call x1, Pallas kernels, per_device(): pl.pallas_call(functools.partial(kernel, n_morton, n_sub), out_shape=(blo...  21.4 us
    pallas_call x1, Pallas kernels, per_device(): pl.pallas_call(finish, out_shape=(shape, shape), in_specs=[vmem, vmem, vm...  0.92 us

profile of v5, /device:TPU:0, one launch (start us, length us, event | category | flops | bytes accessed | tf_op | source)
XLA Modules:
  0.0 22.9 jit_solution(2973721039410803549)
XLA Ops:
  0.6 21.4 %shard_map.122 = (f32[5,128,128]{2,1,0:T(8,128)S(1)}, f32[5,128,128]{2,1,0:T(8,128)S(1)}, f32[5,128,128]{2,1,0:T(8,128)S(1)}) custom-call(f32[5,125,128]{2,1,0:T(8,128)} %state_hbm.1, s32[1,128]{1,0:T(1,128)} %bitcast.5, s32[6,128]{1,0:T(8,128)} %near_hbm.1, s32[1,32]{1,0:T(1,128)} %next_hbm.1, s32[1,32]{1,0:T(1,128)} %prev_hbm.1, s32[1,2,8]{2,1,0:T(2,128)} %bitcast.4, ...), custom_call_target="tpu_custom_call" | custom-call | tf_op jit(solution)/shard_map/pallas_call | solution.py:546
  22.0 0.9 %shard_map.123 = (f32[5,125,128]{2,1,0:T(8,128)}, f32[5,125,128]{2,1,0:T(8,128)}) custom-call(f32[5,128,128]{2,1,0:T(8,128)S(1)} %get-tuple-element.5.x_ref, f32[5,128,128]{2,1,0:T(8,128)S(1)} %get-tuple-element.6.first_ref, f32[5,128,128]{2,1,0:T(8,128)S(1)} %get-tuple-element.7.rate_ref), custom_call_target="tpu_custom_call" | custom-call | tf_op jit(solution)/shard_map/pallas_call | solution.py:580

commit v6 on v5

--- a/solution.py
+++ b/solution.py
@@ -196,6 +196,8 @@
     ring_recv,
     message_send,
     message_recv,
+    relay_ref,
+    relay_sem,
     send_sem,
     recv_sem,
 ):
@@ -212,8 +214,14 @@
     barrier = pltpu.get_barrier_semaphore()
     for o in (4, 3, 5, 2, 6, 1, 7):
         pl.semaphore_signal(barrier, inc=1, device_id=(m, peers[o]), device_id_type=MESH)
-    for target in (after_id, before_id):
-        pl.semaphore_signal(barrier, inc=1, device_id=target, device_id_type=MESH)
+    group_before = (lax.rem(m + n_morton - 1, n_morton), 0)
+    group_after = (lax.rem(m + 1, n_morton), 0)
+
+    @pl.when(s == 0)
+    def greet_groups():
+        for target in (before_id, group_after):
+            pl.semaphore_signal(barrier, inc=1, device_id=target, device_id_type=MESH)
+
 
     loads = [
         pltpu.make_async_copy(source, target, load_sem.at[i])
@@ -340,7 +348,7 @@
         for side in range(2):
             ring_send[step, side] = packed[32 * side : 32 * side + 32, :]
         if step == 0:
-            pl.semaphore_wait(barrier, n_sub + 1)
+            pl.semaphore_wait(barrier, n_sub - 1 + (1 - (s + n_sub - 1) // n_sub) + (s + 1) // n_sub)
         messages = []
         for o in (4,):
             copy = pltpu.make_async_remote_copy(
@@ -363,8 +371,20 @@
                 device_id=target,
                 device_id_type=MESH,
             )
-            copy.start()
             rings.append(copy)
+            if step == 0 and side == 1:
+                relay = pltpu.make_async_remote_copy(
+                    src_ref=ring_send.at[0, 1],
+                    dst_ref=relay_ref,
+                    send_sem=send_sem.at[0, n_sub + 1],
+                    recv_sem=relay_sem.at[0],
+                    device_id=group_before,
+                    device_id_type=MESH,
+                )
+                pl.when(s == 0)(relay.start)
+                pl.when(s > 0)(copy.start)
+            else:
+                copy.start()
         for o in (3, 5, 2, 6, 1, 7):
             copy = pltpu.make_async_remote_copy(
                 src_ref=message_send.at[step, peers[o]],
@@ -452,6 +472,21 @@
         known_parts = mortar_part(known)
         inside = face_fields(inner_ref)
         flux_in, speed_in = flux_by_lane(inside, mortar_part(inside), inner_facts[0])
+        if step == 0:
+            passed_on = pltpu.make_async_remote_copy(
+                src_ref=relay_ref,
+                dst_ref=ring_recv.at[0, 1],
+                send_sem=relay_sem.at[1],
+                recv_sem=recv_sem.at[0, n_sub + 1],
+                device_id=(m, n_sub - 1),
+                device_id_type=MESH,
+            )
+
+            @pl.when(s == 0)
+            def pass_on():
+                relay.wait_recv()
+                passed_on.start()
+
         for copy in rings + messages:
             copy.wait_recv()
         panels = panels_of(message_recv.at[step])
@@ -500,6 +535,8 @@
             for face in range(6):
                 for f in range(5):
                     onto_planes(rate_ref, face, f, gain * added_ref[face, 25 * f : 25 * f + 25, :])
+        if step == 0:
+            pl.when(s == 0)(passed_on.wait_send)
         return rings + messages
 
     copies = section(0)
@@ -570,6 +607,8 @@
             pltpu.VMEM((2, 2, 32, 128), f32),
             pltpu.VMEM((2, n_sub, 10, 128), f32),
             pltpu.VMEM((2, n_sub, 10, 128), f32),
+            pltpu.VMEM((32, 128), f32),
+            pltpu.SemaphoreType.DMA((2,)),
             pltpu.SemaphoreType.DMA((2, n_sub + 2)),
             pltpu.SemaphoreType.DMA((2, n_sub + 2)),
         ],

time: 23 us -> 22.7 us (0.987)
  the two profiles are of different devices: /device:TPU:0 before, /device:TPU:8 now
where the time goes in v6:
time: 22.7 us; the launch traced here: 22.6 us
  Pallas kernels  22 us (97%)
  between operations  0.64 us (3%)
    pallas_call x1, Pallas kernels, per_device(): pl.pallas_call(functools.partial(kernel, n_morton, n_sub), out_shape=(blo...  21.1 us
    pallas_call x1, Pallas kernels, per_device(): pl.pallas_call(finish, out_shape=(shape, shape), in_specs=[vmem, vmem, vm...  0.92 us

profile of v6, /device:TPU:8, one launch (start us, length us, event | category | flops | bytes accessed | tf_op | source)
XLA Modules:
  0.0 22.6 jit_solution(16080868651674214589)
XLA Ops:
  0.6 21.1 %shard_map.122 = (f32[5,128,128]{2,1,0:T(8,128)S(1)}, f32[5,128,128]{2,1,0:T(8,128)S(1)}, f32[5,128,128]{2,1,0:T(8,128)S(1)}) custom-call(f32[5,125,128]{2,1,0:T(8,128)} %state_hbm.1, s32[1,128]{1,0:T(1,128)} %bitcast.5, s32[6,128]{1,0:T(8,128)} %near_hbm.1, s32[1,32]{1,0:T(1,128)} %next_hbm.1, s32[1,32]{1,0:T(1,128)} %prev_hbm.1, s32[1,2,8]{2,1,0:T(2,128)} %bitcast.4, ...), custom_call_target="tpu_custom_call" | custom-call | tf_op jit(solution)/shard_map/pallas_call | solution.py:583
  21.7 0.9 %shard_map.123 = (f32[5,125,128]{2,1,0:T(8,128)}, f32[5,125,128]{2,1,0:T(8,128)}) custom-call(f32[5,128,128]{2,1,0:T(8,128)S(1)} %get-tuple-element.5.x_ref, f32[5,128,128]{2,1,0:T(8,128)S(1)} %get-tuple-element.6.first_ref, f32[5,128,128]{2,1,0:T(8,128)S(1)} %get-tuple-element.7.rate_ref), custom_call_target="tpu_custom_call" | custom-call | tf_op jit(solution)/shard_map/pallas_call | solution.py:619

commit v7 on v6

--- a/solution.py
+++ b/solution.py
@@ -214,14 +214,20 @@
     barrier = pltpu.get_barrier_semaphore()
     for o in (4, 3, 5, 2, 6, 1, 7):
         pl.semaphore_signal(barrier, inc=1, device_id=(m, peers[o]), device_id_type=MESH)
-    group_before = (lax.rem(m + n_morton - 1, n_morton), 0)
-    group_after = (lax.rem(m + 1, n_morton), 0)
+    first_place = place == 0
+    relay_place = place == devices - n_sub
 
     @pl.when(s == 0)
-    def greet_groups():
-        for target in (before_id, group_after):
-            pl.semaphore_signal(barrier, inc=1, device_id=target, device_id_type=MESH)
-
+    def greet_before():
+        pl.semaphore_signal(barrier, inc=1, device_id=before_id, device_id_type=MESH)
+
+    @pl.when((s == n_sub - 1) & (place < devices - 1))
+    def greet_after():
+        pl.semaphore_signal(barrier, inc=1, device_id=after_id, device_id_type=MESH)
+
+    @pl.when(relay_place)
+    def greet_first():
+        pl.semaphore_signal(barrier, inc=1, device_id=(0, 0), device_id_type=MESH)
 
     loads = [
         pltpu.make_async_copy(source, target, load_sem.at[i])
@@ -378,11 +384,11 @@
                     dst_ref=relay_ref,
                     send_sem=send_sem.at[0, n_sub + 1],
                     recv_sem=relay_sem.at[0],
-                    device_id=group_before,
+                    device_id=(n_morton - 1, 0),
                     device_id_type=MESH,
                 )
-                pl.when(s == 0)(relay.start)
-                pl.when(s > 0)(copy.start)
+                pl.when(first_place)(relay.start)
+                pl.when(place > 0)(copy.start)
             else:
                 copy.start()
         for o in (3, 5, 2, 6, 1, 7):
@@ -482,7 +488,7 @@
                 device_id_type=MESH,
             )
 
-            @pl.when(s == 0)
+            @pl.when(relay_place)
             def pass_on():
                 relay.wait_recv()
                 passed_on.start()
@@ -536,7 +542,7 @@
                 for f in range(5):
                     onto_planes(rate_ref, face, f, gain * added_ref[face, 25 * f : 25 * f + 25, :])
         if step == 0:
-            pl.when(s == 0)(passed_on.wait_send)
+            pl.when(relay_place)(passed_on.wait_send)
         return rings + messages
 
     copies = section(0)

time: 22.7 us -> 21.9 us (0.965)
  the two profiles are of different devices: /device:TPU:8 before, /device:TPU:0 now
where the time goes in v7:
time: 21.9 us; the launch traced here: 21.8 us
  Pallas kernels  21.2 us (97%)
  between operations  0.64 us (3%)
    pallas_call x1, Pallas kernels, per_device(): pl.pallas_call(functools.partial(kernel, n_morton, n_sub), out_shape=(blo...  20.3 us
    pallas_call x1, Pallas kernels, per_device(): pl.pallas_call(finish, out_shape=(shape, shape), in_specs=[vmem, vmem, vm...  0.92 us

profile of v7, /device:TPU:0, one launch (start us, length us, event | category | flops | bytes accessed | tf_op | source)
XLA Modules:
  0.0 21.8 jit_solution(12113943207478395175)
XLA Ops:
  0.6 20.3 %shard_map.122 = (f32[5,128,128]{2,1,0:T(8,128)S(1)}, f32[5,128,128]{2,1,0:T(8,128)S(1)}, f32[5,128,128]{2,1,0:T(8,128)S(1)}) custom-call(f32[5,125,128]{2,1,0:T(8,128)} %state_hbm.1, s32[1,128]{1,0:T(1,128)} %bitcast.5, s32[6,128]{1,0:T(8,128)} %near_hbm.1, s32[1,32]{1,0:T(1,128)} %next_hbm.1, s32[1,32]{1,0:T(1,128)} %prev_hbm.1, s32[1,2,8]{2,1,0:T(2,128)} %bitcast.4, ...), custom_call_target="tpu_custom_call" | custom-call | tf_op jit(solution)/shard_map/pallas_call | solution.py:589
  20.9 0.9 %shard_map.123 = (f32[5,125,128]{2,1,0:T(8,128)}, f32[5,125,128]{2,1,0:T(8,128)}) custom-call(f32[5,128,128]{2,1,0:T(8,128)S(1)} %get-tuple-element.5.x_ref, f32[5,128,128]{2,1,0:T(8,128)S(1)} %get-tuple-element.6.first_ref, f32[5,128,128]{2,1,0:T(8,128)S(1)} %get-tuple-element.7.rate_ref), custom_call_target="tpu_custom_call" | custom-call | tf_op jit(solution)/shard_map/pallas_call | solution.py:625

commit v8 on v7

--- a/solution.py
+++ b/solution.py
@@ -349,24 +349,10 @@
             send_pick_ref[...], face_bf_ref[...], across, preferred_element_type=f32
         )
         packed = packed[:, 0:128] + packed[:, 128:256]
-        for p in range(n_sub):
-            message_send[step, p] = packed[64 + 16 * p : 74 + 16 * p, :]
         for side in range(2):
             ring_send[step, side] = packed[32 * side : 32 * side + 32, :]
         if step == 0:
             pl.semaphore_wait(barrier, n_sub - 1 + (1 - (s + n_sub - 1) // n_sub) + (s + 1) // n_sub)
-        messages = []
-        for o in (4,):
-            copy = pltpu.make_async_remote_copy(
-                src_ref=message_send.at[step, peers[o]],
-                dst_ref=message_recv.at[step, s],
-                send_sem=send_sem.at[step, o],
-                recv_sem=recv_sem.at[step, o],
-                device_id=(m, peers[o]),
-                device_id_type=MESH,
-            )
-            copy.start()
-            messages.append(copy)
         rings = []
         for side, target in enumerate((after_id, before_id)):
             copy = pltpu.make_async_remote_copy(
@@ -391,6 +377,20 @@
                 pl.when(place > 0)(copy.start)
             else:
                 copy.start()
+        for p in range(n_sub):
+            message_send[step, p] = packed[64 + 16 * p : 74 + 16 * p, :]
+        messages = []
+        for o in (4,):
+            copy = pltpu.make_async_remote_copy(
+                src_ref=message_send.at[step, peers[o]],
+                dst_ref=message_recv.at[step, s],
+                send_sem=send_sem.at[step, o],
+                recv_sem=recv_sem.at[step, o],
+                device_id=(m, peers[o]),
+                device_id_type=MESH,
+            )
+            copy.start()
+            messages.append(copy)
         for o in (3, 5, 2, 6, 1, 7):
             copy = pltpu.make_async_remote_copy(
                 src_ref=message_send.at[step, peers[o]],

time: 21.9 us -> 21.9 us (level)
  no operation moved by 1% of the time
where the time goes in v8:
time: 21.9 us; the launch traced here: 21.8 us
  Pallas kernels  21.2 us (97%)
  between operations  0.64 us (3%)
    pallas_call x1, Pallas kernels, per_device(): pl.pallas_call(functools.partial(kernel, n_morton, n_sub), out_shape=(blo...  20.2 us
    pallas_call x1, Pallas kernels, per_device(): pl.pallas_call(finish, out_shape=(shape, shape), in_specs=[vmem, vmem, vm...  0.92 us

profile of v8, /device:TPU:0, one launch (start us, length us, event | category | flops | bytes accessed | tf_op | source)
XLA Modules:
  0.0 21.8 jit_solution(6811977731553994108)
XLA Ops:
  0.6 20.2 %shard_map.122 = (f32[5,128,128]{2,1,0:T(8,128)S(1)}, f32[5,128,128]{2,1,0:T(8,128)S(1)}, f32[5,128,128]{2,1,0:T(8,128)S(1)}) custom-call(f32[5,125,128]{2,1,0:T(8,128)} %state_hbm.1, s32[1,128]{1,0:T(1,128)} %bitcast.5, s32[6,128]{1,0:T(8,128)} %near_hbm.1, s32[1,32]{1,0:T(1,128)} %next_hbm.1, s32[1,32]{1,0:T(1,128)} %prev_hbm.1, s32[1,2,8]{2,1,0:T(2,128)} %bitcast.4, ...), custom_call_target="tpu_custom_call" | custom-call | tf_op jit(solution)/shard_map/pallas_call | solution.py:589
  20.9 0.9 %shard_map.123 = (f32[5,125,128]{2,1,0:T(8,128)}, f32[5,125,128]{2,1,0:T(8,128)}) custom-call(f32[5,128,128]{2,1,0:T(8,128)S(1)} %get-tuple-element.5.x_ref, f32[5,128,128]{2,1,0:T(8,128)S(1)} %get-tuple-element.6.first_ref, f32[5,128,128]{2,1,0:T(8,128)S(1)} %get-tuple-element.7.rate_ref), custom_call_target="tpu_custom_call" | custom-call | tf_op jit(solution)/shard_map/pallas_call | solution.py:625
